TPU v7x, 32 devices: a whole 2x2x4 slice. The times are simulated.
32 devices in a mesh: seq: 8 (over y, x, core), mp: 4 (over z).
Axes of the slice: x: 2, y: 2, z: 4, core: 2. Of those that a mesh axis runs over, the one named last changes fastest.
Arguments:
- byte_states: bfloat16 [4096, 1024], P('seq'), may hold values from -6 to 6
- patch_starts: int32 [8, 192], P('seq'), may hold values from 0 to 512, as said below
- patch_counts: int32 [8, 1], P('seq'), may hold values from 64 to 192, as said below
- patch_owner: int32 [8, 192], P('seq'), may hold values from -1 to 7, as said below
- enc_query: bfloat16 [1024, 1024], P(None, 'mp'), may hold values from -0.1875 to 0.1875
- enc_key: bfloat16 [1024, 1024], P(None, 'mp'), may hold values from -0.1875 to 0.1875
- enc_value: bfloat16 [1024, 1024], P(None, 'mp'), may hold values from -0.1875 to 0.1875
- enc_out: bfloat16 [1024, 4096], P('mp'), may hold values from -0.1875 to 0.1875
- up_proj: bfloat16 [4096, 7168], P('seq', 'mp'), may hold values from -0.09375 to 0.09375
- down_proj: bfloat16 [4096, 7168], P('seq', 'mp'), may hold values from -0.0625 to 0.0625
- dec_query: bfloat16 [1024, 1024], P(None, 'mp'), may hold values from -0.1875 to 0.1875
- dec_key: bfloat16 [4096, 1024], P(None, 'mp'), may hold values from -0.09375 to 0.09375
- dec_value: bfloat16 [4096, 1024], P(None, 'mp'), may hold values from -0.09375 to 0.09375
- dec_out: bfloat16 [1024, 1024], P('mp'), may hold values from -0.1875 to 0.1875
- latent_cotangent: bfloat16 [1536, 4096], P('seq', 'mp'), may hold values from -6 to 6
Outputs:
- decoded: bfloat16 [4096, 1024], P('seq', 'mp')
- patch_grad: bfloat16 [1536, 4096], P('seq', 'mp')
- down_grad: bfloat16 [4096, 7168], P('seq', 'mp')
Inputs may be any that keep to these rules, and one draw needn't show every extreme that they name: `patch_counts`: the counts of all shards sum to 128 times the number of shards; some shard has exactly 192 patches and some exactly 64. `patch_starts`: in each shard's row the first entry is 0, the first count entries rise strictly and stay below 512, and the remaining entries equal 512. `patch_owner`: entries at or beyond the shard's count are -1, the others name a latent shard. Every latent shard owns exactly 128 patches in all and at most 24 of one byte shard's patches; a shard with 192 patches gives exactly 24 to every latent shard.
All inputs are finite; a program needn't handle non-finite values.
Results may differ from a plain program's by a relative error of at most 0.024.
Values may be sent and summed in bfloat16 or wider, within the bound.
No kernel may reach another device: no remote copies, remote signals or barrier semaphores. Data moves between devices by JAX's collectives and lax.ppermute only.
A program may use at most 128 MiB of HBM per device.

v0:
```python
import math

import jax
import jax.numpy as jnp
from jax import lax
from jax.experimental import pallas as pl
from jax.experimental.pallas import tpu as pltpu
from jax.sharding import PartitionSpec as P

HD = 64
CAP = 128
MASKED = -1e30


BF = jnp.bfloat16
F32 = jnp.float32


def gelu_back(hidden_pre, incoming):
    return jax.vjp(jax.nn.gelu, hidden_pre)[1](incoming)[0]


def attend(queries, keys_in, values_in, allowed, head_count):
    row_count = queries.shape[0]
    col_count = keys_in.shape[0]
    head_width = queries.shape[1] // head_count
    query_heads = queries.reshape(row_count, head_count, head_width)
    key_heads = keys_in.reshape(col_count, head_count, head_width)
    value_heads = values_in.reshape(col_count, head_count, head_width)
    scores = (
        jnp.einsum("rhd,chd->hrc", query_heads, key_heads, preferred_element_type=F32)
        / head_width**0.5
    )
    scores = jnp.where(allowed[None], scores, MASKED)
    weights = jax.nn.softmax(scores, axis=-1).astype(BF)
    mixed = jnp.einsum("hrc,chd->rhd", weights, value_heads, preferred_element_type=F32)
    return mixed.reshape(row_count, head_count * head_width).astype(BF)


def dot(left, right):
    return jnp.dot(left, right, preferred_element_type=F32)


def contract_last(left, right):
    return lax.dot_general(left, right, (((1,), (1,)), ((), ())), preferred_element_type=F32)


def contract_first(left, right):
    return lax.dot_general(left, right, (((0,), (0,)), ((), ())), preferred_element_type=F32)


def seq_swap(value, bits):
    return lax.ppermute(value, "seq", [(i, i ^ bits) for i in range(lax.axis_size("seq"))])


def mp_swap(value, bits):
    return lax.ppermute(value, "mp", [(i, i ^ bits) for i in range(lax.axis_size("mp"))])


def gather_mp(value):
    return [value] + [mp_swap(value, k) for k in range(1, lax.axis_size("mp"))]


def exchange_mp(pieces):
    return [pieces[0]] + [mp_swap(pieces[k], k) for k in range(1, len(pieces))]


def gather_seq(value):
    out = []
    for chip in range(lax.axis_size("seq") // 2):
        same = value if chip == 0 else seq_swap(value, 2 * chip)
        out += [same, seq_swap(same, 1)]
    return out


def exchange_seq(blocks):
    chips = blocks.shape[0]
    got = [blocks[0]] + [seq_swap(blocks[i], 2 * i) for i in range(1, chips)]
    mine = jnp.stack([piece[0] for piece in got])
    other = seq_swap(jnp.stack([piece[1] for piece in got]), 1)
    return jnp.stack([mine, other], axis=1)


def scatter_sum_seq(partial):
    size = lax.axis_size("seq")
    here = lax.axis_index("seq")
    rows = partial.shape[0] // size

    def block(j):
        return lax.dynamic_slice_in_dim(partial, (here ^ j) * rows, rows, 0)

    total = None
    for chip in list(range(1, size // 2)) + [0]:
        arrived = seq_swap(block(2 * chip + 1), 1)
        summed = block(2 * chip).astype(F32) + arrived.astype(F32)
        if chip:
            summed = seq_swap(summed.astype(BF), 2 * chip).astype(F32)
        total = summed if total is None else total + summed
    return total


def place_rows(blocks):
    here = lax.axis_index("seq")
    rows = blocks[0].shape[0]
    out = jnp.zeros((rows * len(blocks), blocks[0].shape[1]), blocks[0].dtype)
    for j, block in enumerate(blocks):
        out = lax.dynamic_update_slice_in_dim(out, block, (here ^ j) * rows, 0)
    return out


def call_on_blocks(body, scalars, operands, outs, scratch, flops, moved):
    whole = pl.BlockSpec(memory_space=pltpu.VMEM)
    return pl.pallas_call(
        body,
        out_shape=outs,
        in_specs=[pl.BlockSpec(memory_space=pltpu.SMEM)] + [whole] * len(operands),
        out_specs=[whole] * len(outs),
        scratch_shapes=scratch,
        compiler_params=pltpu.CompilerParams(vmem_limit_bytes=48 * 1024 * 1024),
        cost_estimate=pl.CostEstimate(flops=flops, bytes_accessed=moved, transcendentals=0),
    )(scalars, *operands)


def block_rows(total, most):
    best = total
    for step in range(16, most + 1, 16):
        if total % step == 0:
            best = step
    return best


def partial_blocks(weight_t, wide, lane_index=None):
    size = lax.axis_size("seq")
    rows = weight_t.shape[0] // size
    depth = weight_t.shape[1]
    chips = size // 2
    piece_rows, sub = wide[0].shape
    by_columns = lane_index is not None
    width = piece_rows if by_columns else piece_rows * len(wide)

    def body(place_ref, low_ref, high_ref, *refs):
        count = len(wide)
        wide_refs, mine_ref, other_ref = refs[:count], refs[count], refs[count + 1]
        if by_columns:
            right_ref = refs[count + 2]

            @pl.when(pl.program_id(0) == 0)
            def _():
                for k, wide_ref in enumerate(wide_refs):
                    start = pl.multiple_of((place_ref[1] ^ k) * sub, sub)
                    right_ref[:, pl.ds(start, sub)] = wide_ref[...]

            wide_refs = [right_ref]
        for left_ref, out_ref in ((low_ref, mine_ref), (high_ref, other_ref)):
            left = left_ref[...]
            for n, wide_ref in enumerate(wide_refs):
                out_ref[0, :, n * piece_rows : (n + 1) * piece_rows] = contract_last(
                    left, wide_ref[...]
                ).astype(BF)

    lane = lane_index if by_columns else lax.axis_index("mp")
    place = jnp.stack([lax.axis_index("seq"), lane]).astype(jnp.int32)
    spec = pltpu.PrefetchScalarGridSpec(
        num_scalar_prefetch=1,
        grid=(chips,),
        in_specs=[
            pl.BlockSpec((rows, depth), lambda i, place: (place[0] ^ (2 * i), 0)),
            pl.BlockSpec((rows, depth), lambda i, place: (place[0] ^ (2 * i + 1), 0)),
        ]
        + [pl.BlockSpec((piece_rows, sub), lambda i, place: (0, 0))] * len(wide),
        out_specs=[pl.BlockSpec((1, rows, width), lambda i, place: (i, 0, 0))] * 2,
        scratch_shapes=[pltpu.VMEM((width, depth), BF)] if by_columns else [],
    )
    shape = jax.ShapeDtypeStruct((chips, rows, width), BF)
    return pl.pallas_call(
        body,
        grid_spec=spec,
        out_shape=[shape, shape],
        compiler_params=pltpu.CompilerParams(vmem_limit_bytes=32 * 1024 * 1024),
        cost_estimate=pl.CostEstimate(
            flops=2 * size * rows * width * depth,
            bytes_accessed=2 * size * rows * (width + depth),
            transcendentals=0,
        ),
    )(place, weight_t, weight_t, *wide)


def add_halves(mine, other):
    chips, rows, width = mine.shape
    step = block_rows(rows, 64)

    def body(mine_ref, other_ref, *out_refs):
        for i, out_ref in enumerate(out_refs):
            total = mine_ref[i].astype(F32) + other_ref[i].astype(F32)
            out_ref[...] = total.astype(out_ref.dtype)

    whole = pl.BlockSpec((chips, step, width), lambda r: (0, r, 0))
    return pl.pallas_call(
        body,
        grid=(rows // step,),
        in_specs=[whole, whole],
        out_specs=[pl.BlockSpec((step, width), lambda r: (r, 0))] * chips,
        out_shape=[
            jax.ShapeDtypeStruct((rows, width), BF if i else F32) for i in range(chips)
        ],
        cost_estimate=pl.CostEstimate(
            flops=mine.size, bytes_accessed=8 * mine.size, transcendentals=0
        ),
    )(mine, other)


def scatter_blocks(mine, other):
    arrived = seq_swap(other, 1)
    summed = add_halves(mine, arrived)
    got = [seq_swap(summed[i], 2 * i) for i in range(1, len(summed))]
    total = summed[0]
    for piece in got:
        total = total + piece.astype(F32)
    return total


def sort_cot(got, count, lane_index):
    lanes = len(got)
    per_lane, slots, sub = got[0].shape
    chips = lanes * per_lane // 2

    def body(table_ref, *refs):
        got_refs, out_refs = refs[:lanes], refs[lanes:]
        for i, out_ref in enumerate(out_refs):
            for t in range(2):
                place = table_ref[0] ^ (2 * i + t)
                source = (place // per_lane) ^ table_ref[1]
                value = got_refs[0][place % per_lane]
                for k in range(1, lanes):
                    value = jnp.where(source == k, got_refs[k][place % per_lane], value)
                out_ref[t, :slots, :] = value
                out_ref[t, slots:, :] = jnp.full((16, sub), table_ref[2].astype(F32)).astype(BF)

    table = jnp.stack([lax.axis_index("seq"), lane_index, count]).astype(jnp.int32)
    out = jax.ShapeDtypeStruct((2, slots + 16, sub), BF)
    return call_on_blocks(body, table, got, [out] * chips, [], 0, 8 * chips * slots * sub)


def exchange_pieces(blocks):
    mine = [blocks[0]] + [seq_swap(blocks[i], 2 * i) for i in range(1, len(blocks))]
    return mine, [seq_swap(piece, 1) for piece in mine]


def pack_cot(mine, other, total_rows):
    chips = len(mine)
    size = 2 * chips
    sub = mine[0].shape[2]
    slots = mine[0].shape[1] - 16

    def body(place_ref, *refs):
        mine_refs, other_refs = refs[:chips], refs[chips:size]
        packed_ref, table_ref = refs[size:]
        blocks = [(refs_of[j // 2], j % 2) for j, refs_of in enumerate([mine_refs, other_refs] * chips)]
        counts = [ref[t, slots : slots + 1, 0:1].astype(F32) for ref, t in blocks]
        row = lax.broadcasted_iota(jnp.int32, (total_rows, slots), 0)
        slot = lax.broadcasted_iota(jnp.int32, (total_rows, slots), 1)
        gap = (row - slot).astype(F32)
        slot = slot.astype(F32)
        total = jnp.zeros((total_rows, sub), F32)
        for j, (ref, t) in enumerate(blocks):
            offset = jnp.zeros((1, 1), F32)
            for n in range(size):
                before = (place_ref[0] ^ n) < (place_ref[0] ^ j)
                offset = offset + jnp.where(before, counts[n], 0.0)
            spread = jnp.where((gap == offset) & (slot < counts[j]), 1.0, 0.0).astype(BF)
            total = total + dot(spread, ref[t, :slots, :])
            table_ref[j : j + 1, :] = jnp.broadcast_to(offset, (1, 128)).astype(jnp.int32)
            table_ref[size + j : size + j + 1, :] = jnp.broadcast_to(counts[j], (1, 128)).astype(
                jnp.int32
            )
        packed_ref[...] = total.astype(BF)

    place = lax.axis_index("seq").astype(jnp.int32)[None]
    packed, table = call_on_blocks(
        body,
        place,
        mine + other,
        [
            jax.ShapeDtypeStruct((total_rows, sub), BF),
            jax.ShapeDtypeStruct((2 * size, 128), jnp.int32),
        ],
        [],
        2 * size * slots * total_rows * sub,
        8 * size * slots * sub,
    )
    return packed, table[:, 0]


def hidden_kernel(lifted, mixed, enc_pieces, table, lane_index, total_rows, sub):
    rows = lifted.shape[0]
    slots = mixed[0].shape[0]
    size = len(mixed)
    piece = enc_pieces[0].shape[0]

    def body(table_ref, lifted_ref, *refs):
        mixed_refs, enc_refs = refs[:size], refs[size : size + len(enc_pieces)]
        pre_ref, hidden_ref, rows_ref, stack_ref, spread_ref = refs[size + len(enc_pieces) :]
        lane = pl.multiple_of(table_ref[2 * size] * sub, sub)
        left = lifted_ref[...]
        slot = lax.broadcasted_iota(jnp.int32, (slots, total_rows), 0)
        gap = lax.broadcasted_iota(jnp.int32, (slots, total_rows), 1) - slot
        for j in range(size):
            spread_ref[j * slots : (j + 1) * slots, :] = jnp.where(
                (gap == table_ref[j]) & (slot < table_ref[size + j]), 1.0, 0.0
            ).astype(BF)
        for i in range(size // 2):
            slot_pre = jnp.concatenate(
                [contract_last(left, mixed_refs[2 * i + t][...]) for t in range(2)], axis=1
            )
            high = slot_pre.astype(BF)
            columns = slice(2 * i * slots, 2 * (i + 1) * slots)
            stack_ref[:rows, columns] = jax.nn.gelu(slot_pre).astype(BF)
            stack_ref[rows : 2 * rows, columns] = high
            stack_ref[2 * rows :, columns] = (slot_pre - high.astype(F32)).astype(BF)
        hidden_ref[...] = dot(stack_ref[:rows, :], spread_ref[...]).astype(BF)
        pre_ref[...] = dot(stack_ref[rows : 2 * rows, :], spread_ref[...]) + dot(
            stack_ref[2 * rows :, :], spread_ref[...]
        )
        for j, mixed_ref in enumerate(mixed_refs):
            patch = jnp.zeros((slots, sub), F32)
            for n, enc_ref in enumerate(enc_refs):
                patch = patch + dot(
                    mixed_ref[:, n * piece : (n + 1) * piece], enc_ref[:, pl.ds(lane, sub)]
                )
            rows_ref[j * slots : (j + 1) * slots, :] = patch.astype(BF)

    table = jnp.concatenate([table, lane_index.astype(jnp.int32)[None]])
    width = lifted.shape[1]
    return call_on_blocks(
        body,
        table,
        [lifted] + mixed + enc_pieces,
        [
            jax.ShapeDtypeStruct((rows, total_rows), F32),
            jax.ShapeDtypeStruct((rows, total_rows), BF),
            jax.ShapeDtypeStruct((size * slots, sub), BF),
        ],
        [pltpu.VMEM((3 * rows, size * slots), BF), pltpu.VMEM((size * slots, total_rows), BF)],
        2 * size * slots * (rows * (width + 3 * total_rows) + width * sub),
        2 * (size * slots * width + 3 * rows * total_rows),
    )


def unpack_home(parts, rows_own, table, slots):
    count = len(parts)
    size = table.shape[0] // 2
    total_rows, sub = parts[0].shape
    extra = [] if rows_own is None else [rows_own]

    def body(table_ref, *refs):
        total = refs[0][...].astype(F32)
        for ref in refs[1:count]:
            total = total + ref[...].astype(F32)
        total = total.astype(BF)
        slot = lax.broadcasted_iota(jnp.int32, (slots, total_rows), 0)
        gap = lax.broadcasted_iota(jnp.int32, (slots, total_rows), 1) - slot
        outs = refs[count + len(extra) :]
        for j in range(size):
            live = slot < table_ref[size + j]
            spread = jnp.where((gap == table_ref[j]) & live, 1.0, 0.0).astype(BF)
            home = dot(spread, total)
            if extra:
                own = refs[count][j * slots : (j + 1) * slots, :].astype(F32)
                home = home + jnp.where(live[:, :sub], own, 0.0)
            outs[j // 2][j % 2] = home.astype(BF)

    out = jax.ShapeDtypeStruct((2, slots, sub), BF)
    return call_on_blocks(
        body,
        table,
        parts + extra,
        [out] * (size // 2),
        [],
        2 * size * slots * total_rows * sub,
        2 * (count * total_rows + 2 * size * slots) * sub,
    )


def keys_values(mine, other, weights, lanes):
    chips = len(mine)
    _, slots, sub = mine[0].shape
    width = weights[0].shape[2]

    def body(place_ref, *refs):
        mine_refs, other_refs, weight_refs = refs[:chips], refs[chips : 2 * chips], refs[2 * chips : 4 * chips]
        out_refs = refs[4 * chips :]
        for k, out_ref in enumerate(out_refs):
            total = jnp.zeros((slots, width), F32)
            for j, weight_ref in enumerate(weight_refs):
                ref = (mine_refs, other_refs)[j % 2][j // 2]
                total = total + dot(ref[j % 2], weight_ref[k])
            out_ref[...] = total.astype(BF)

    return call_on_blocks(
        body,
        jnp.zeros((1,), jnp.int32),
        mine + other + weights,
        [jax.ShapeDtypeStruct((slots, width), BF)] * lanes,
        [],
        4 * chips * slots * sub * lanes * width,
        4 * chips * sub * lanes * width,
    )


def sort_grad(mine, other, lanes, lane_index):
    chips = len(mine)
    _, slots, sub = mine[0].shape
    per_lane = 2 * chips // lanes

    def body(place_ref, *refs):
        mine_refs, other_refs = refs[:chips], refs[chips : 2 * chips]
        for k, out_ref in enumerate(refs[2 * chips :]):
            for p in range(per_lane):
                place = ((place_ref[1] ^ k) * per_lane + p) ^ place_ref[0]
                value = mine_refs[0][0]
                for j in range(1, 2 * chips):
                    block = (mine_refs, other_refs)[j % 2][j // 2][j % 2]
                    value = jnp.where(place == j, block, value)
                out_ref[p] = value

    place = jnp.stack([lax.axis_index("seq"), lane_index]).astype(jnp.int32)
    out = jax.ShapeDtypeStruct((per_lane, slots, sub), BF)
    return call_on_blocks(body, place, mine + other, [out] * lanes, [], 0, 8 * chips * slots * sub)


def finish_grad(cot, got, count, lane_index):
    lanes = len(got)
    per_lane, slots, sub = got[0].shape

    def body(place_ref, cot_ref, *refs):
        live = lax.broadcasted_iota(jnp.int32, (slots, sub), 0) < place_ref[1]
        for k in range(lanes):
            for p in range(per_lane):
                columns = pl.ds(pl.multiple_of((p * lanes + (place_ref[0] ^ k)) * sub, sub), sub)
                total = cot_ref[:, columns].astype(F32) + refs[k][p].astype(F32)
                refs[lanes][:, columns] = jnp.where(live, total, 0.0).astype(BF)

    place = jnp.stack([lane_index, count]).astype(jnp.int32)
    return call_on_blocks(
        body, place, [cot] + got, [jax.ShapeDtypeStruct(cot.shape, BF)], [], 0, 6 * cot.size
    )[0]


def mix_pieces(pieces, weight_t, lane_index):
    size = len(pieces)
    lanes = lax.axis_size("mp")
    rows, total_rows = pieces[0].shape
    width = weight_t.shape[1]
    sub = width // lanes
    step = 256 if total_rows % 256 == 0 else total_rows

    def body(place_ref, weight_ref, *refs):
        piece_refs, out_refs, acc_ref = refs[:size], refs[size:-1], refs[-1]
        total = None
        for j, piece_ref in enumerate(piece_refs):
            start = pl.multiple_of((place_ref[0] ^ j) * rows, 16)
            part = contract_first(piece_ref[...], weight_ref[pl.ds(start, rows), :])
            total = part if total is None else total + part
        acc_ref[...] = total
        for k, out_ref in enumerate(out_refs):
            start = pl.multiple_of((place_ref[1] ^ k) * sub, sub)
            out_ref[...] = acc_ref[:, pl.ds(start, sub)].astype(BF)

    place = jnp.stack([lax.axis_index("seq"), lane_index]).astype(jnp.int32)
    spec = pltpu.PrefetchScalarGridSpec(
        num_scalar_prefetch=1,
        grid=(total_rows // step,),
        in_specs=[pl.BlockSpec(weight_t.shape, lambda r, place: (0, 0))]
        + [pl.BlockSpec((rows, step), lambda r, place: (0, r))] * size,
        out_specs=[pl.BlockSpec((step, sub), lambda r, place: (r, 0))] * lanes,
        scratch_shapes=[pltpu.VMEM((step, width), F32)],
    )
    return pl.pallas_call(
        body,
        grid_spec=spec,
        out_shape=[jax.ShapeDtypeStruct((total_rows, sub), BF)] * lanes,
        compiler_params=pltpu.CompilerParams(vmem_limit_bytes=32 * 1024 * 1024),
        cost_estimate=pl.CostEstimate(
            flops=2 * size * rows * total_rows * width,
            bytes_accessed=2 * (size * rows * (total_rows + width) + total_rows * width),
            transcendentals=0,
        ),
    )(place, weight_t, *pieces)


def outer_pieces(cot_lanes, pieces, lane_index, scale):
    size = len(pieces)
    lanes = len(cot_lanes)
    rows, total_rows = pieces[0].shape
    sub = cot_lanes[0].shape[1]
    full = size * rows
    step = block_rows(full, 256) if full % 256 else 256

    def body(place_ref, *refs):
        cot_refs, piece_refs = refs[:lanes], refs[lanes : lanes + size]
        out_ref, acc_ref = refs[lanes + size :]
        for j, piece_ref in enumerate(piece_refs):
            start = pl.multiple_of((place_ref[0] ^ j) * rows, 16)
            left = piece_ref[...]
            for k, cot_ref in enumerate(cot_refs):
                acc_ref[pl.ds(start, rows), k * sub : (k + 1) * sub] = dot(left, cot_ref[...]) * scale
        for k in range(lanes):
            top = pl.multiple_of((place_ref[1] ^ k) * sub, sub)
            for n in range(full // step):
                block = acc_ref[n * step : (n + 1) * step, k * sub : (k + 1) * sub]
                out_ref[pl.ds(top, sub), n * step : (n + 1) * step] = block.T.astype(BF)

    place = jnp.stack([lax.axis_index("seq"), lane_index]).astype(jnp.int32)
    return call_on_blocks(
        body,
        place,
        cot_lanes + pieces,
        [jax.ShapeDtypeStruct((lanes * sub, full), BF)],
        [pltpu.VMEM((full, lanes * sub), F32)],
        2 * full * total_rows * lanes * sub,
        2 * (full * total_rows + total_rows * lanes * sub + full * lanes * sub),
    )[0]


def per_device(
    byte_states,
    patch_starts,
    patch_counts,
    patch_owner,
    enc_query,
    enc_key,
    enc_value,
    enc_out,
    up_proj,
    down_proj,
    dec_query,
    dec_key,
    dec_value,
    dec_out,
    latent_cotangent,
):
    groups = lax.axis_size("seq")
    chips = groups // 2
    lanes = lax.axis_size("mp")
    here = lax.axis_index("seq")
    lane_index = lax.axis_index("mp")
    byte_count = byte_states.shape[0]
    slots = patch_starts.shape[1]
    total_rows = groups * CAP
    slice_width = up_proj.shape[0]
    sub = slice_width // lanes
    per_lane = groups // lanes
    patch_start = patch_starts[0]
    patch_total = patch_counts[0, 0]
    hidden_rows = up_proj.shape[1] // groups
    tiled = hidden_rows % 16 == 0 and sub % 128 == 0 and slots % 64 == 0 and groups <= 8
    scale = 1.0 / math.sqrt(total_rows)
    relative = jnp.arange(groups, dtype=jnp.int32) ^ here
    slot_ids = jnp.arange(slots, dtype=jnp.int32)
    positions = jnp.arange(byte_count, dtype=jnp.int32)

    enc_own = lax.dynamic_slice_in_dim(enc_out, here * slice_width, slice_width, 1)
    enc_pieces = gather_mp(enc_own)

    def cot_piece(k):
        return jnp.stack(
            [
                lax.dynamic_slice_in_dim(
                    latent_cotangent, (p * lanes + (lane_index ^ k)) * sub, sub, 1
                )
                for p in range(per_lane)
            ]
        )

    cot_got = exchange_mp([cot_piece(k) for k in range(lanes)])

    patch_end = jnp.concatenate([patch_start[1:], jnp.full((1,), byte_count, jnp.int32)])
    member = (positions[None, :] >= patch_start[:, None]) & (
        positions[None, :] < patch_end[:, None]
    )
    lengths = jnp.sum(member.astype(F32), axis=1)
    pooled = dot(member.astype(BF), byte_states)
    pooled = (pooled / jnp.maximum(lengths, 1.0)[:, None]).astype(BF)
    queries = dot(pooled, enc_query).astype(BF)
    keys_in = dot(byte_states, enc_key).astype(BF)
    values_in = dot(byte_states, enc_value).astype(BF)

    if tiled:
        up_t = up_proj.T
        keys_in, values_in, up_later = lax.optimization_barrier((keys_in, values_in, up_t))
        lifted_parts = partial_blocks(up_later, enc_pieces)
        cot_sent = sort_cot(cot_got, patch_total, lane_index)
        cot_mine, cot_other = exchange_pieces(cot_sent)
        cot_packed, table = pack_cot(cot_mine, cot_other, total_rows)
    else:
        enc_slice = jnp.concatenate(enc_pieces, axis=0)
        lifted_part = lax.dot_general(
            up_proj, enc_slice, (((0,), (1,)), ((), ())), preferred_element_type=F32
        ).astype(BF)
        lifted = scatter_sum_seq(lifted_part).astype(BF)
        cot_sent = jnp.full((groups, slots + 16, sub), patch_total.astype(F32).astype(BF))
        for k in range(lanes):
            for p in range(per_lane):
                place = ((lane_index ^ k) * per_lane + p) ^ here
                cot_sent = lax.dynamic_update_slice(cot_sent, cot_got[k][p][None], (place, 0, 0))
        cot_here = exchange_seq(cot_sent.reshape(chips, 2, slots + 16, sub)).reshape(
            groups, slots + 16, sub
        )
        counts = cot_here[:, slots, 0].astype(F32).astype(jnp.int32)
        before = relative[None, :] < relative[:, None]
        offsets = jnp.sum(jnp.where(before, counts[None, :], 0), axis=1)
        places = jnp.where(
            slot_ids[None, :] < counts[:, None], offsets[:, None] + slot_ids[None, :], -1
        ).reshape(groups * slots)
        row_ids = jnp.arange(total_rows, dtype=jnp.int32)
        selector = (row_ids[:, None] == places[None, :]).astype(BF)
        cot_packed = dot(selector, cot_here[:, :slots].reshape(groups * slots, sub)).astype(BF)

    cot_all = gather_mp(cot_packed)
    if not tiled:
        cot_slice = jnp.zeros((total_rows, slice_width), BF)
        for k in range(lanes):
            cot_slice = lax.dynamic_update_slice_in_dim(
                cot_slice, cot_all[k], (lane_index ^ k) * sub, 1
            )

    if tiled:
        queries, *lifted_parts = lax.optimization_barrier((queries, *lifted_parts))
    mixed = attend(queries, keys_in, values_in, member, enc_query.shape[1] // HD)
    if tiled:
        lifted = scatter_blocks(*lifted_parts).astype(BF)
    mixed = jnp.concatenate(gather_mp(mixed), axis=1)
    mixed_pieces = gather_seq(mixed)

    def sum_parts(got):
        total = got[0].astype(F32)
        for piece in got[1:]:
            total = total + piece.astype(F32)
        return total

    rows_of = lambda weight, k: lax.dynamic_slice_in_dim(
        weight, here * slice_width + (lane_index ^ k) * sub, sub, 0
    )
    head_pieces = exchange_mp(
        [
            jnp.concatenate([rows_of(dec_key, k), rows_of(dec_value, k)], axis=1)
            for k in range(lanes)
        ]
    )
    head_weights = jnp.stack(head_pieces)
    head_weights = gather_seq(head_weights)

    if tiled:
        hidden_pre, hidden, rows_own = hidden_kernel(
            lifted, mixed_pieces, enc_pieces, table, lane_index, total_rows, sub
        )
        hidden_pieces = gather_seq(hidden)
        down_later, _ = lax.optimization_barrier((down_proj, cot_packed))
        down_t = down_later.T
        forward_blocks = mix_pieces(hidden_pieces, down_t, lane_index)
        forward_got = exchange_mp(forward_blocks)
        down_grad = outer_pieces(cot_all, hidden_pieces, lane_index, scale)
        backward_parts = partial_blocks(down_t, cot_all, lane_index)
        backward = scatter_blocks(*backward_parts)
        inner = gelu_back(hidden_pre, backward).astype(BF)
        inner_pieces = gather_seq(inner)
        backward_blocks = mix_pieces(inner_pieces, up_t, lane_index)
        backward_got = exchange_mp(backward_blocks)
        latent_sent = unpack_home(forward_got, rows_own, table, slots)
        latent_mine, latent_other = exchange_pieces(latent_sent)
        terms = keys_values(latent_mine, latent_other, head_weights, lanes)
    else:
        mixed_all = jnp.concatenate(mixed_pieces, axis=0)
        slot_pre = contract_last(lifted, mixed_all)
        slot_hidden = jax.nn.gelu(slot_pre).astype(BF)
        hidden = contract_last(slot_hidden, selector).astype(BF)
        hidden_all = place_rows(gather_seq(hidden))
        forward_part = lax.dot_general(
            hidden_all, down_proj, (((0,), (1,)), ((), ())), preferred_element_type=F32
        ).astype(BF)
        pre_high = slot_pre.astype(BF)
        pre_low = (slot_pre - pre_high.astype(F32)).astype(BF)
        hidden_pre = contract_last(pre_high, selector) + contract_last(pre_low, selector)
        backward_partial = lax.dot_general(
            down_proj, cot_slice, (((0,), (1,)), ((), ())), preferred_element_type=F32
        ).astype(BF)
        backward = scatter_sum_seq(backward_partial)
        inner = gelu_back(hidden_pre, backward).astype(BF)
        inner_all = place_rows(gather_seq(inner))
        backward_part = lax.dot_general(
            inner_all, up_proj, (((0,), (1,)), ((), ())), preferred_element_type=F32
        ).astype(BF)
        down_grad = lax.dot_general(
            cot_slice, hidden_all, (((0,), (1,)), ((), ())), preferred_element_type=F32
        )
        down_grad = (down_grad * scale).astype(BF)

        def sum_lanes(part):
            blocks = [
                lax.dynamic_slice_in_dim(part, (lane_index ^ k) * sub, sub, 1) for k in range(lanes)
            ]
            return sum_parts(exchange_mp(blocks)).astype(BF)

        def send_home(home):
            return exchange_seq(home.astype(BF).reshape(chips, 2, slots, sub)).reshape(
                groups, slots, sub
            )

        enc_sub = lax.dynamic_slice_in_dim(enc_slice, lane_index * sub, sub, 1)
        rows_own = jnp.where((places >= 0)[:, None], dot(mixed_all, enc_sub), 0.0)
        latent_here = send_home(contract_first(selector, sum_lanes(forward_part)) + rows_own)
        terms = []
        for k in range(lanes):
            term = sum(dot(latent_here[j], head_weights[j][k]) for j in range(groups))
            terms.append(term.astype(BF))

    terms = exchange_mp(terms)
    both = sum_parts(terms).astype(BF)
    dec_queries = dot(byte_states, dec_query).astype(BF)
    dec_keys = both[:, : dec_key.shape[1]]
    dec_values = both[:, dec_key.shape[1] :]
    home_patch = (
        jnp.sum((patch_start[None, :] <= positions[:, None]).astype(jnp.int32), axis=1) - 1
    )
    allowed = slot_ids[None, :] <= home_patch[:, None]
    byte_mixed = attend(dec_queries, dec_keys, dec_values, allowed, dec_query.shape[1] // HD)
    decoded_part = dot(byte_mixed, dec_out).astype(BF)
    width_here = decoded_part.shape[1] // lanes
    got = exchange_mp(
        [
            lax.dynamic_slice_in_dim(decoded_part, (lane_index ^ k) * width_here, width_here, 1)
            for k in range(lanes)
        ]
    )
    own_cols = lax.dynamic_slice_in_dim(byte_states, lane_index * width_here, width_here, 1)
    decoded = (own_cols.astype(F32) + sum_parts(got)).astype(BF)

    if tiled:
        grad_sent = unpack_home(backward_got, None, table, slots)
        grad_mine, grad_other = exchange_pieces(grad_sent)
        grad_out = sort_grad(grad_mine, grad_other, lanes, lane_index)
        grad_got = exchange_mp(grad_out)
        patch_grad = finish_grad(latent_cotangent, grad_got, patch_total, lane_index)
        return (decoded, patch_grad, down_grad)

    grad_here = send_home(contract_first(selector, sum_lanes(backward_part)))

    def grad_piece(k):
        return jnp.stack(
            [
                lax.dynamic_index_in_dim(
                    grad_here, ((lane_index ^ k) * per_lane + p) ^ here, 0, keepdims=False
                )
                for p in range(per_lane)
            ]
        )

    grad_got = exchange_mp([grad_piece(k) for k in range(lanes)])
    grad_cols = jnp.zeros((slots, lanes * per_lane * sub), BF)
    for k in range(lanes):
        for p in range(per_lane):
            grad_cols = lax.dynamic_update_slice_in_dim(
                grad_cols, grad_got[k][p], (p * lanes + (lane_index ^ k)) * sub, 1
            )
    live = patch_owner[0] >= 0
    patch_grad = latent_cotangent.astype(F32) + grad_cols.astype(F32)
    patch_grad = jnp.where(live[:, None], patch_grad, 0.0).astype(BF)
    return (decoded, patch_grad, down_grad)


def solution(mesh):
    return jax.shard_map(
        per_device,
        mesh=mesh,
        in_specs=(
            P("seq", None),
            P("seq", None),
            P("seq", None),
            P("seq", None),
            P(None, "mp"),
            P(None, "mp"),
            P(None, "mp"),
            P("mp", None),
            P("seq", "mp"),
            P("seq", "mp"),
            P(None, "mp"),
            P(None, "mp"),
            P(None, "mp"),
            P("mp", None),
            P("seq", "mp"),
        ),
        out_specs=(P("seq", "mp"), P("seq", "mp"), P("seq", "mp")),
        check_vma=False,
    )
```

profile of v0, /device:TPU:0, one launch (start us, length us, event | category | flops | bytes accessed | tf_op | source)
XLA Modules:
  0.0 346.5 jit_solution(11238062521658570129)
XLA Ops:
  20.1 7.0 %collective-permute-done.1.refs_2_ = bf16[2,192,128]{2,1,0:T(8,128)(2,1)S(1)} collective-permute-done((bf16[2,192,128]{2,1,0:T(8,128)(2,1)S(1)}, bf16[2,192,128]{2,1,0:T(8,128)(2,1)S(1)}, u32[]{:S(2)}, u32[]{:S(2)}) %collective-permute-start.1) | collective-permute-done | bytes 98336 | tf_op jit(solution)/shard_map/ppermute | solution.py:57
  49.4 5.6 %shard_map.159 = (bf16[4,224,1024]{2,1,0:T(8,128)(2,1)S(1)}, bf16[4,224,1024]{2,1,0:T(8,128)(2,1)}) custom-call(s32[2]{0:T(128)S(1)} %pad_add_fusion.2.place_ref, bf16[1792,512]{1,0:T(8,128)(2,1)S(1)} %bitcast.60, bf16[1792,512]{1,0:T(8,128)(2,1)S(1)} %bitcast.61, bf16[256,512]{1,0:T(8,128)(2,1)S(1)} %constant_dynamic-slice_fusion.11.refs_0_.refs_8_, ...), custom_call_target="tpu_custom_call" | custom-call | flops 1879048192 | bytes 5505024 | tf_op jit(solution)/shard_map/pallas_call | solution.py:175
  60.2 7.7 %collective-permute-done.61.refs_2_ = bf16[1024,128]{1,0:T(8,128)(2,1)S(1)} collective-permute-done((bf16[1024,128]{1,0:T(8,128)(2,1)S(1)}, bf16[1024,128]{1,0:T(8,128)(2,1)S(1)}, u32[]{:S(2)}, u32[]{:S(2)}) %collective-permute-start.61) | collective-permute-done | bytes 262176 | tf_op jit(solution)/shard_map/ppermute | solution.py:57
  69.6 4.8 %shard_map.165 = (bf16[4,224,1024]{2,1,0:T(8,128)(2,1)S(1)}, bf16[4,224,1024]{2,1,0:T(8,128)(2,1)}) custom-call(s32[2]{0:T(128)S(1)} %pad_add_fusion.2.place_ref, bf16[1792,512]{1,0:T(8,128)(2,1)S(1)} %bitcast.63, bf16[1792,512]{1,0:T(8,128)(2,1)S(1)} %bitcast.64, bf16[1024,128]{1,0:T(8,128)(2,1)S(1)} %get-tuple-element.60.refs_0_, ...), custom_call_target="tpu_custom_call" | custom-call | flops 1879048192 | bytes 5505024 | tf_op jit(solution)/shard_map/pallas_call | solution.py:175
  86.8 6.1 %collective-permute-done.18 = bf16[192,256]{1,0:T(8,128)(2,1)S(1)} collective-permute-done((bf16[192,256]{1,0:T(8,128)(2,1)S(1)}, bf16[192,256]{1,0:T(8,128)(2,1)S(1)}, u32[]{:S(2)}, u32[]{:S(2)}) %collective-permute-start.18) | collective-permute-done | bytes 98336 | tf_op jit(solution)/shard_map/ppermute | solution.py:57
  96.3 5.6 %collective-permute-done.46 = bf16[128,512]{1,0:T(8,128)(2,1)S(1)} collective-permute-done((bf16[128,512]{1,0:T(8,128)(2,1)S(1)}, bf16[128,512]{1,0:T(8,128)(2,1)S(1)}, u32[]{:S(2)}, u32[]{:S(2)}) %collective-permute-start.46) | collective-permute-done | bytes 131104 | tf_op jit(solution)/shard_map/ppermute | solution.py:57
  109.8 5.6 %shard_map.160 = (f32[224,1024]{1,0:T(8,128)}, bf16[224,1024]{1,0:T(8,128)(2,1)}, bf16[224,1024]{1,0:T(8,128)(2,1)}, bf16[224,1024]{1,0:T(8,128)(2,1)}) custom-call(bf16[4,224,1024]{2,1,0:T(8,128)(2,1)} %copy-done.5, bf16[4,224,1024]{2,1,0:T(8,128)(2,1)} %collective-permute-done.13.other_ref), custom_call_target="tpu_custom_call" | custom-call | flops 917504 | bytes 7340032 | tf_op jit(solution)/shard_map/pallas_call | solution.py:198
  115.4 10.2 %collective-permute-done.23.refs_4_ = bf16[192,1024]{1,0:T(8,128)(2,1)S(1)} collective-permute-done((bf16[192,1024]{1,0:T(8,128)(2,1)S(1)}, bf16[192,1024]{1,0:T(8,128)(2,1)S(1)}, u32[]{:S(2)}, u32[]{:S(2)}) %collective-permute-start.23) | collective-permute-done | bytes 393248 | tf_op jit(solution)/shard_map/ppermute | solution.py:53
  130.9 5.6 %shard_map.166 = (f32[224,1024]{1,0:T(8,128)}, bf16[224,1024]{1,0:T(8,128)(2,1)}, bf16[224,1024]{1,0:T(8,128)(2,1)}, bf16[224,1024]{1,0:T(8,128)(2,1)}) custom-call(bf16[4,224,1024]{2,1,0:T(8,128)(2,1)} %copy-done.4, bf16[4,224,1024]{2,1,0:T(8,128)(2,1)} %collective-permute-done.63.other_ref), custom_call_target="tpu_custom_call" | custom-call | flops 917504 | bytes 7340032 | tf_op jit(solution)/shard_map/pallas_call | solution.py:198
  141.3 8.4 %collective-permute-done.15 = bf16[224,1024]{1,0:T(8,128)(2,1)} collective-permute-done((bf16[224,1024]{1,0:T(8,128)(2,1)}, bf16[224,1024]{1,0:T(8,128)(2,1)}, u32[]{:S(2)}, u32[]{:S(2)}) %collective-permute-start.15) | collective-permute-done | bytes 458784 | tf_op jit(solution)/shard_map/ppermute | solution.py:53
  154.6 7.1 %shard_map.161 = (f32[224,1024]{1,0:T(8,128)}, bf16[224,1024]{1,0:T(8,128)(2,1)S(1)}, bf16[1536,128]{1,0:T(8,128)(2,1)S(1)}) custom-call(s32[17]{0:T(128)S(1)} %pad_add_fusion.3.table_ref, bf16[224,1024]{1,0:T(8,128)(2,1)S(1)} %add_convert_fusion.lifted_ref, bf16[192,1024]{1,0:T(8,128)(2,1)S(1)} %copy-done.18, ...), custom_call_target="tpu_custom_call" | custom-call | flops 3221225472 | bytes 4521984 | tf_op jit(solution)/shard_map/pallas_call | solution.py:113
  164.4 8.7 %collective-permute-done.52.refs_14_ = bf16[4,128,512]{2,1,0:T(8,128)(2,1)S(1)} collective-permute-done((bf16[4,128,512]{2,1,0:T(8,128)(2,1)S(1)}, bf16[4,128,512]{2,1,0:T(8,128)(2,1)S(1)}, u32[]{:S(2)}, u32[]{:S(2)}) %collective-permute-start.52) | collective-permute-done | bytes 524320 | tf_op jit(solution)/shard_map/ppermute | solution.py:53
  173.6 9.2 %collective-permute-done.66 = bf16[224,1024]{1,0:T(8,128)(2,1)S(1)} collective-permute-done((bf16[224,1024]{1,0:T(8,128)(2,1)}, bf16[224,1024]{1,0:T(8,128)(2,1)S(1)}, u32[]{:S(2)}, u32[]{:S(2)}) %collective-permute-start.66) | collective-permute-done | bytes 458784 | tf_op jit(solution)/shard_map/ppermute | solution.py:53
  184.3 7.5 %collective-permute-done.65 = bf16[224,1024]{1,0:T(8,128)(2,1)S(1)} collective-permute-done((bf16[224,1024]{1,0:T(8,128)(2,1)S(1)}, bf16[224,1024]{1,0:T(8,128)(2,1)S(1)}, u32[]{:S(2)}, u32[]{:S(2)}) %collective-permute-start.65) | collective-permute-done | bytes 458784 | tf_op jit(solution)/shard_map/ppermute | solution.py:53
  192.3 9.2 %collective-permute-done.64 = bf16[224,1024]{1,0:T(8,128)(2,1)S(1)} collective-permute-done((bf16[224,1024]{1,0:T(8,128)(2,1)S(1)}, bf16[224,1024]{1,0:T(8,128)(2,1)S(1)}, u32[]{:S(2)}, u32[]{:S(2)}) %collective-permute-start.64) | collective-permute-done | bytes 458784 | tf_op jit(solution)/shard_map/ppermute | solution.py:53
  202.4 9.0 %collective-permute-done.32.refs_6_.refs_10_ = bf16[224,1024]{1,0:T(8,128)(2,1)S(1)} collective-permute-done((bf16[224,1024]{1,0:T(8,128)(2,1)S(1)}, bf16[224,1024]{1,0:T(8,128)(2,1)S(1)}, u32[]{:S(2)}, u32[]{:S(2)}) %collective-permute-start.32) | collective-permute-done | bytes 458784 | tf_op jit(solution)/shard_map/ppermute | solution.py:53
  217.7 4.4 %shard_map.162 = (bf16[1024,128]{1,0:T(8,128)(2,1)S(1)}, bf16[1024,128]{1,0:T(8,128)(2,1)S(1)}, bf16[1024,128]{1,0:T(8,128)(2,1)S(1)}, bf16[1024,128]{1,0:T(8,128)(2,1)S(1)}) custom-call(s32[2]{0:T(128)S(1)} %pad_add_fusion.2.place_ref, bf16[1792,512]{1,0:T(8,128)(2,1)S(1)} %bitcast.65, bf16[224,1024]{1,0:T(8,128)(2,1)S(1)} %get-tuple-element.74.refs_0_.refs_4_, ...), custom_call_target="tpu_custom_call" | custom-call | flops 1879048192 | bytes 6553600 | tf_op jit(solution)/shard_map/pallas_call | solution.py:478
  230.0 7.7 %collective-permute-done.70.refs_4_ = bf16[224,1024]{1,0:T(8,128)(2,1)S(1)} collective-permute-done((bf16[224,1024]{1,0:T(8,128)(2,1)S(1)}, bf16[224,1024]{1,0:T(8,128)(2,1)S(1)}, u32[]{:S(2)}, u32[]{:S(2)}) %collective-permute-start.70) | collective-permute-done | bytes 458784 | tf_op jit(solution)/shard_map/ppermute | solution.py:53
  238.3 5.4 %collective-permute-done.35.refs_2_ = bf16[1024,128]{1,0:T(8,128)(2,1)S(1)} collective-permute-done((bf16[1024,128]{1,0:T(8,128)(2,1)S(1)}, bf16[1024,128]{1,0:T(8,128)(2,1)S(1)}, u32[]{:S(2)}, u32[]{:S(2)}) %collective-permute-start.35) | collective-permute-done | bytes 262176 | tf_op jit(solution)/shard_map/ppermute | solution.py:57
  250.7 5.1 %shard_map.167 = (bf16[1024,128]{1,0:T(8,128)(2,1)S(1)}, bf16[1024,128]{1,0:T(8,128)(2,1)}, bf16[1024,128]{1,0:T(8,128)(2,1)S(1)}, bf16[1024,128]{1,0:T(8,128)(2,1)S(1)}) custom-call(s32[2]{0:T(128)S(1)} %pad_add_fusion.2.place_ref, bf16[1792,512]{1,0:T(8,128)(2,1)S(1)} %bitcast.62, bf16[224,1024]{1,0:T(8,128)(2,1)S(1)} %fusion.15.refs_0_, ...), custom_call_target="tpu_custom_call" | custom-call | flops 1879048192 | bytes 6553600 | tf_op jit(solution)/shard_map/pallas_call | solution.py:478
  280.1 14.3 %collective-permute-done.75.refs_2_ = bf16[1024,128]{1,0:T(8,128)(2,1)S(1)} collective-permute-done((bf16[1024,128]{1,0:T(8,128)(2,1)}, bf16[1024,128]{1,0:T(8,128)(2,1)S(1)}, u32[]{:S(2)}, u32[]{:S(2)}) %collective-permute-start.75) | collective-permute-done | bytes 262176 | tf_op jit(solution)/shard_map/ppermute | solution.py:57
  299.6 8.2 %collective-permute-done.55 = bf16[192,512]{1,0:T(8,128)(2,1)S(1)} collective-permute-done((bf16[192,512]{1,0:T(8,128)(2,1)S(1)}, bf16[192,512]{1,0:T(8,128)(2,1)S(1)}, u32[]{:S(2)}, u32[]{:S(2)}) %collective-permute-start.55) | collective-permute-done | bytes 196640 | tf_op jit(solution)/shard_map/ppermute | solution.py:57
  320.1 14.1 %collective-permute-done.84.refs_1_ = bf16[2,192,128]{2,1,0:T(8,128)(2,1)S(1)} collective-permute-done((bf16[2,192,128]{2,1,0:T(8,128)(2,1)S(1)}, bf16[2,192,128]{2,1,0:T(8,128)(2,1)S(1)}, u32[]{:S(2)}, u32[]{:S(2)}) %collective-permute-start.84) | collective-permute-done | bytes 98336 | tf_op jit(solution)/shard_map/ppermute | solution.py:57
  335.8 6.3 %shard_map.171 = bf16[512,1792]{1,0:T(8,128)(2,1)} custom-call(s32[2]{0:T(128)S(1)} %pad_add_fusion.2.place_ref, bf16[1024,128]{1,0:T(8,128)(2,1)S(1)} %copy-done.42, bf16[1024,128]{1,0:T(8,128)(2,1)S(1)} %copy-done.44, bf16[1024,128]{1,0:T(8,128)(2,1)S(1)} %copy-done.46, bf16[1024,128]{1,0:T(8,128)(2,1)S(1)} %copy-done.48, ...), custom_call_target="tpu_custom_call" | custom-call | flops 1879048192 | bytes 6553600 | tf_op jit(solution)/shard_map/pallas_call | solution.py:113
  (354 shorter events, 161.2 us)
Async XLA Ops:
  2.3 45.8 %collective-permute-start.10 = (bf16[256,512]{1,0:T(8,128)(2,1)S(1)}, bf16[256,512]{1,0:T(8,128)(2,1)S(1)}, u32[]{:S(2)}, u32[]{:S(2)}) collective-permute-start(bf16[256,512]{1,0:T(8,128)(2,1)S(1)} %constant_dynamic-slice_fusion.11.refs_0_.refs_8_), channel_id=1, source_target_pairs={{0,1},{1,0},{2,3},{3,2},{4,5},{5,4},{6,7},{7,6},{8,9},{9,8},{10,11... | collective-permute-start | bytes 786440 | tf_op jit(solution)/shard_map/ppermute | solution.py:57
  5.4 44.0 %collective-permute-start.11 = (bf16[256,512]{1,0:T(8,128)(2,1)S(1)}, bf16[256,512]{1,0:T(8,128)(2,1)}, u32[]{:S(2)}, u32[]{:S(2)}) collective-permute-start(bf16[256,512]{1,0:T(8,128)(2,1)S(1)} %constant_dynamic-slice_fusion.11.refs_0_.refs_8_), channel_id=1, source_target_pairs={{0,2},{1,3},{2,0},{3,1},{4,6},{5,7},{6,4},{7,5},{8,10},{9,11},{10,... | collective-permute-start | bytes 786440 | tf_op jit(solution)/shard_map/ppermute | solution.py:57
  56.4 52.9 %collective-permute-start.13 = (bf16[4,224,1024]{2,1,0:T(8,128)(2,1)}, bf16[4,224,1024]{2,1,0:T(8,128)(2,1)}, u32[]{:S(2)}, u32[]{:S(2)}) collective-permute-start(bf16[4,224,1024]{2,1,0:T(8,128)(2,1)} %get-tuple-element.66), channel_id=1, source_target_pairs={{0,4},{4,0},{8,12},{12,8},{16,20},{20,16},{24,28},{28,24},{1,5},{5... | collective-permute-start | bytes 5505032 | tf_op jit(solution)/shard_map/ppermute | solution.py:53
  75.7 53.4 %collective-permute-start.63 = (bf16[4,224,1024]{2,1,0:T(8,128)(2,1)}, bf16[4,224,1024]{2,1,0:T(8,128)(2,1)}, u32[]{:S(2)}, u32[]{:S(2)}) collective-permute-start(bf16[4,224,1024]{2,1,0:T(8,128)(2,1)} %get-tuple-element.89), channel_id=1, source_target_pairs={{0,4},{4,0},{8,12},{12,8},{16,20},{20,16},{24,28},{28,24},{1,5},{5... | collective-permute-start | bytes 5505032 | tf_op jit(solution)/shard_map/ppermute | solution.py:53
  136.5 25.1 %collective-permute-start.47 = (bf16[4,128,512]{2,1,0:T(8,128)(2,1)S(1)}, bf16[4,128,512]{2,1,0:T(8,128)(2,1)S(1)}, u32[]{:S(2)}, u32[]{:S(2)}) collective-permute-start(bf16[4,128,512]{2,1,0:T(8,128)(2,1)S(1)} %pad_maximum_fusion.refs_8_), channel_id=1, source_target_pairs={{0,4},{4,0},{8,12},{12,8},{16,20},{20,16},{24,28},{28,24},{1,5},{5... | collective-permute-start | bytes 1572872 | tf_op jit(solution)/shard_map/ppermute | solution.py:53
  136.6 25.7 %collective-permute-start.48 = (bf16[4,128,512]{2,1,0:T(8,128)(2,1)S(1)}, bf16[4,128,512]{2,1,0:T(8,128)(2,1)S(1)}, u32[]{:S(2)}, u32[]{:S(2)}) collective-permute-start(bf16[4,128,512]{2,1,0:T(8,128)(2,1)S(1)} %pad_maximum_fusion.refs_8_), channel_id=1, source_target_pairs={{0,8},{4,12},{8,0},{12,4},{16,24},{20,28},{24,16},{28,20},{1,9},{5... | collective-permute-start | bytes 1572872 | tf_op jit(solution)/shard_map/ppermute | solution.py:53
  140.7 23.0 %collective-permute-start.50 = (bf16[4,128,512]{2,1,0:T(8,128)(2,1)S(1)}, bf16[4,128,512]{2,1,0:T(8,128)(2,1)S(1)}, u32[]{:S(2)}, u32[]{:S(2)}) collective-permute-start(bf16[4,128,512]{2,1,0:T(8,128)(2,1)S(1)} %pad_maximum_fusion.refs_8_), channel_id=1, source_target_pairs={{0,16},{4,20},{8,24},{12,28},{16,0},{20,4},{24,8},{28,12},{1,17},{... | collective-permute-start | bytes 1572872 | tf_op jit(solution)/shard_map/ppermute | solution.py:53
  149.7 23.3 %collective-permute-start.52 = (bf16[4,128,512]{2,1,0:T(8,128)(2,1)S(1)}, bf16[4,128,512]{2,1,0:T(8,128)(2,1)S(1)}, u32[]{:S(2)}, u32[]{:S(2)}) collective-permute-start(bf16[4,128,512]{2,1,0:T(8,128)(2,1)S(1)} %pad_maximum_fusion.refs_8_), channel_id=1, source_target_pairs={{0,24},{4,28},{8,16},{12,20},{16,8},{20,12},{24,0},{28,4},{1,25},{... | collective-permute-start | bytes 1572872 | tf_op jit(solution)/shard_map/ppermute | solution.py:53
  151.2 31.6 %collective-permute-start.66 = (bf16[224,1024]{1,0:T(8,128)(2,1)}, bf16[224,1024]{1,0:T(8,128)(2,1)S(1)}, u32[]{:S(2)}, u32[]{:S(2)}) collective-permute-start(bf16[224,1024]{1,0:T(8,128)(2,1)} %get-tuple-element.93), channel_id=1, source_target_pairs={{0,24},{4,28},{8,16},{12,20},{16,8},{20,12},{24,0},{28,4},{1,25},{... | collective-permute-start | bytes 1376264 | tf_op jit(solution)/shard_map/ppermute | solution.py:53
  161.7 30.1 %collective-permute-start.65 = (bf16[224,1024]{1,0:T(8,128)(2,1)S(1)}, bf16[224,1024]{1,0:T(8,128)(2,1)S(1)}, u32[]{:S(2)}, u32[]{:S(2)}) collective-permute-start(bf16[224,1024]{1,0:T(8,128)(2,1)S(1)} %copy-done.69), channel_id=1, source_target_pairs={{0,16},{4,20},{8,24},{12,28},{16,0},{20,4},{24,8},{28,12},{1,17},{... | collective-permute-start | bytes 1376264 | tf_op jit(solution)/shard_map/ppermute | solution.py:53
  162.3 29.5 %collective-permute-start.28 = (bf16[224,1024]{1,0:T(8,128)(2,1)S(1)}, bf16[224,1024]{1,0:T(8,128)(2,1)S(1)}, u32[]{:S(2)}, u32[]{:S(2)}) collective-permute-start(bf16[224,1024]{1,0:T(8,128)(2,1)S(1)} %get-tuple-element.74.refs_0_.refs_4_), channel_id=1, source_target_pairs={{0,8},{4,12},{8,0},{12,4},{16,24},{20,28},{24,16},{28,20},{1,9},{5... | collective-permute-start | bytes 1376264 | tf_op jit(solution)/shard_map/ppermute | solution.py:53
  163.8 37.8 %collective-permute-start.64 = (bf16[224,1024]{1,0:T(8,128)(2,1)S(1)}, bf16[224,1024]{1,0:T(8,128)(2,1)S(1)}, u32[]{:S(2)}, u32[]{:S(2)}) collective-permute-start(bf16[224,1024]{1,0:T(8,128)(2,1)S(1)} %copy-done.68), channel_id=1, source_target_pairs={{0,8},{4,12},{8,0},{12,4},{16,24},{20,28},{24,16},{28,20},{1,9},{5... | collective-permute-start | bytes 1376264 | tf_op jit(solution)/shard_map/ppermute | solution.py:53
  173.0 29.3 %collective-permute-start.30 = (bf16[224,1024]{1,0:T(8,128)(2,1)S(1)}, bf16[224,1024]{1,0:T(8,128)(2,1)S(1)}, u32[]{:S(2)}, u32[]{:S(2)}) collective-permute-start(bf16[224,1024]{1,0:T(8,128)(2,1)S(1)} %get-tuple-element.74.refs_0_.refs_4_), channel_id=1, source_target_pairs={{0,16},{4,20},{8,24},{12,28},{16,0},{20,4},{24,8},{28,12},{1,17},{... | collective-permute-start | bytes 1376264 | tf_op jit(solution)/shard_map/ppermute | solution.py:53
  182.8 28.6 %collective-permute-start.32 = (bf16[224,1024]{1,0:T(8,128)(2,1)S(1)}, bf16[224,1024]{1,0:T(8,128)(2,1)S(1)}, u32[]{:S(2)}, u32[]{:S(2)}) collective-permute-start(bf16[224,1024]{1,0:T(8,128)(2,1)S(1)} %get-tuple-element.74.refs_0_.refs_4_), channel_id=1, source_target_pairs={{0,24},{4,28},{8,16},{12,20},{16,8},{20,12},{24,0},{28,4},{1,25},{... | collective-permute-start | bytes 1376264 | tf_op jit(solution)/shard_map/ppermute | solution.py:53
  191.8 22.3 %collective-permute-start.29 = (bf16[224,1024]{1,0:T(8,128)(2,1)S(1)}, bf16[224,1024]{1,0:T(8,128)(2,1)S(1)}, u32[]{:S(2)}, u32[]{:S(2)}) collective-permute-start(bf16[224,1024]{1,0:T(8,128)(2,1)S(1)} %collective-permute-done.28.refs_2_.refs_6_), channel_id=1, source_target_pairs={{0,4},{4,0},{8,12},{12,8},{16,20},{20,16},{24,28},{28,24},{1,5},{5... | collective-permute-start | bytes 1376264 | tf_op jit(solution)/shard_map/ppermute | solution.py:53
  264.3 30.0 %collective-permute-start.75 = (bf16[1024,128]{1,0:T(8,128)(2,1)}, bf16[1024,128]{1,0:T(8,128)(2,1)S(1)}, u32[]{:S(2)}, u32[]{:S(2)}) collective-permute-start(bf16[1024,128]{1,0:T(8,128)(2,1)} %copy-done.52), channel_id=1, source_target_pairs={{0,2},{1,3},{2,0},{3,1},{4,6},{5,7},{6,4},{7,5},{8,10},{9,11},{10,... | collective-permute-start | bytes 786440 | tf_op jit(solution)/shard_map/ppermute | solution.py:57
  265.6 28.8 %collective-permute-start.76 = (bf16[1024,128]{1,0:T(8,128)(2,1)}, bf16[1024,128]{1,0:T(8,128)(2,1)S(1)}, u32[]{:S(2)}, u32[]{:S(2)}) collective-permute-start(bf16[1024,128]{1,0:T(8,128)(2,1)} %copy-done.51), channel_id=1, source_target_pairs={{0,3},{1,2},{2,1},{3,0},{4,7},{5,6},{6,5},{7,4},{8,11},{9,10},{10,... | collective-permute-start | bytes 786440 | tf_op jit(solution)/shard_map/ppermute | solution.py:57
  275.6 22.5 %collective-permute-start.56 = (bf16[192,512]{1,0:T(8,128)(2,1)S(1)}, bf16[192,512]{1,0:T(8,128)(2,1)S(1)}, u32[]{:S(2)}, u32[]{:S(2)}) collective-permute-start(bf16[192,512]{1,0:T(8,128)(2,1)S(1)} %get-tuple-element.87), channel_id=1, source_target_pairs={{0,3},{1,2},{2,1},{3,0},{4,7},{5,6},{6,5},{7,4},{8,11},{9,10},{10,... | collective-permute-start | bytes 589832 | tf_op jit(solution)/shard_map/ppermute | solution.py:57
  277.5 30.2 %collective-permute-start.55 = (bf16[192,512]{1,0:T(8,128)(2,1)S(1)}, bf16[192,512]{1,0:T(8,128)(2,1)S(1)}, u32[]{:S(2)}, u32[]{:S(2)}) collective-permute-start(bf16[192,512]{1,0:T(8,128)(2,1)S(1)} %get-tuple-element.86), channel_id=1, source_target_pairs={{0,2},{1,3},{2,0},{3,1},{4,6},{5,7},{6,4},{7,5},{8,10},{9,11},{10,... | collective-permute-start | bytes 589832 | tf_op jit(solution)/shard_map/ppermute | solution.py:57
  277.5 30.2 %collective-permute-start.54 = (bf16[192,512]{1,0:T(8,128)(2,1)S(1)}, bf16[192,512]{1,0:T(8,128)(2,1)S(1)}, u32[]{:S(2)}, u32[]{:S(2)}) collective-permute-start(bf16[192,512]{1,0:T(8,128)(2,1)S(1)} %get-tuple-element.85), channel_id=1, source_target_pairs={{0,1},{1,0},{2,3},{3,2},{4,5},{5,4},{6,7},{7,6},{8,9},{9,8},{10,11... | collective-permute-start | bytes 589832 | tf_op jit(solution)/shard_map/ppermute | solution.py:57
  311.6 33.0 %collective-permute-start.59 = (bf16[512,256]{1,0:T(8,128)(2,1)S(1)}, bf16[512,256]{1,0:T(8,128)(2,1)S(1)}, u32[]{:S(2)}, u32[]{:S(2)}) collective-permute-start(bf16[512,256]{1,0:T(8,128)(2,1)S(1)} %get-tuple-element.116), channel_id=1, source_target_pairs={{0,3},{1,2},{2,1},{3,0},{4,7},{5,6},{6,5},{7,4},{8,11},{9,10},{10,... | collective-permute-start | bytes 786440 | tf_op jit(solution)/shard_map/ppermute | solution.py:57
  314.1 30.5 %collective-permute-start.58 = (bf16[512,256]{1,0:T(8,128)(2,1)S(1)}, bf16[512,256]{1,0:T(8,128)(2,1)S(1)}, u32[]{:S(2)}, u32[]{:S(2)}) collective-permute-start(bf16[512,256]{1,0:T(8,128)(2,1)S(1)} %get-tuple-element.117), channel_id=1, source_target_pairs={{0,2},{1,3},{2,0},{3,1},{4,6},{5,7},{6,4},{7,5},{8,10},{9,11},{10,... | collective-permute-start | bytes 786440 | tf_op jit(solution)/shard_map/ppermute | solution.py:57
  314.1 30.5 %collective-permute-start.57 = (bf16[512,256]{1,0:T(8,128)(2,1)S(1)}, bf16[512,256]{1,0:T(8,128)(2,1)S(1)}, u32[]{:S(2)}, u32[]{:S(2)}) collective-permute-start(bf16[512,256]{1,0:T(8,128)(2,1)S(1)} %get-tuple-element.115), channel_id=1, source_target_pairs={{0,1},{1,0},{2,3},{3,2},{4,5},{5,4},{6,7},{7,6},{8,9},{9,8},{10,11... | collective-permute-start | bytes 786440 | tf_op jit(solution)/shard_map/ppermute | solution.py:57
  317.3 25.8 %collective-permute-start.85 = (bf16[2,192,128]{2,1,0:T(8,128)(2,1)S(1)}, bf16[2,192,128]{2,1,0:T(8,128)(2,1)S(1)}, u32[]{:S(2)}, u32[]{:S(2)}) collective-permute-start(bf16[2,192,128]{2,1,0:T(8,128)(2,1)S(1)} %get-tuple-element.105), channel_id=1, source_target_pairs={{0,2},{1,3},{2,0},{3,1},{4,6},{5,7},{6,4},{7,5},{8,10},{9,11},{10,... | collective-permute-start | bytes 294920 | tf_op jit(solution)/shard_map/ppermute | solution.py:57
  (133 other events, 1901.5 us)
where the time goes:
time: 348 us; the launch traced here: 346 us
  waiting for transfers between devices  154 us (44%)
  starting transfers between devices  90.1 us (26%)
  Pallas kernels  55.1 us (16%)
  local copies, waits for them, and re-layouts  26.4 us (8%)
  matrix products  10.4 us (3%)
  other arithmetic  8.13 us (2%)
    ppermute x57, waiting for transfers between devices, seq_swap(): lax.ppermute(value, 'seq', [(i, i ^ bits) for i in range(lax.axis_size('s...  79.6 us
    ppermute x30, waiting for transfers between devices, mp_swap(): lax.ppermute(value, 'mp', [(i, i ^ bits) for i in range(lax.axis_size('mp...  74.5 us
    ppermute x30, starting transfers between devices, mp_swap(): lax.ppermute(value, 'mp', [(i, i ^ bits) for i in range(lax.axis_size('mp...  54.3 us
    ppermute x57, starting transfers between devices, seq_swap(): lax.ppermute(value, 'seq', [(i, i ^ bits) for i in range(lax.axis_size('s...  35.8 us
    pallas_call x9, Pallas kernels, call_on_blocks(): pl.pallas_call(body, out_shape=outs, in_specs=[pl.BlockSpec(memory_space=...  24 us
    unnamed x141, local copies, waits for them, and re-layouts  18.5 us
    pallas_call x2, Pallas kernels, add_halves(): pl.pallas_call(body, grid=(rows // step,), in_specs=[whole, whole], out_s...  11.2 us
    pallas_call x2, Pallas kernels, partial_blocks(): pl.pallas_call(body, grid_spec=spec, out_shape=[shape, shape], compiler_p...  10.4 us
  transfers between devices with their start and end apart: 87, of which 27 were waited for; matrix products, arithmetic and copies ran while one was open for 8% of the time, Pallas kernels for 16%

commit v1 on v0

--- a/solution.py
+++ b/solution.py
@@ -187,7 +187,7 @@
 
 def add_halves(mine, other):
     chips, rows, width = mine.shape
-    step = block_rows(rows, 64)
+    step = block_rows(rows, 128)
 
     def body(mine_ref, other_ref, *out_refs):
         for i, out_ref in enumerate(out_refs):
@@ -203,6 +203,7 @@
         out_shape=[
             jax.ShapeDtypeStruct((rows, width), BF if i else F32) for i in range(chips)
         ],
+        compiler_params=pltpu.CompilerParams(vmem_limit_bytes=32 * 1024 * 1024),
         cost_estimate=pl.CostEstimate(
             flops=mine.size, bytes_accessed=8 * mine.size, transcendentals=0
         ),
@@ -213,8 +214,12 @@
     arrived = seq_swap(other, 1)
     summed = add_halves(mine, arrived)
     got = [seq_swap(summed[i], 2 * i) for i in range(1, len(summed))]
-    total = summed[0]
-    for piece in got:
+    return [summed[0]] + got
+
+
+def sum_parts(got):
+    total = got[0].astype(F32)
+    for piece in got[1:]:
         total = total + piece.astype(F32)
     return total
 
@@ -292,16 +297,18 @@
 
 
 def hidden_kernel(lifted, mixed, enc_pieces, table, lane_index, total_rows, sub):
-    rows = lifted.shape[0]
+    terms = len(lifted)
+    rows, width = lifted[0].shape
     slots = mixed[0].shape[0]
     size = len(mixed)
     piece = enc_pieces[0].shape[0]
 
-    def body(table_ref, lifted_ref, *refs):
+    def body(table_ref, *refs):
+        lifted_refs, refs = refs[:terms], refs[terms:]
         mixed_refs, enc_refs = refs[:size], refs[size : size + len(enc_pieces)]
         pre_ref, hidden_ref, rows_ref, stack_ref, spread_ref = refs[size + len(enc_pieces) :]
         lane = pl.multiple_of(table_ref[2 * size] * sub, sub)
-        left = lifted_ref[...]
+        left = sum_parts([ref[...] for ref in lifted_refs]).astype(BF)
         slot = lax.broadcasted_iota(jnp.int32, (slots, total_rows), 0)
         gap = lax.broadcasted_iota(jnp.int32, (slots, total_rows), 1) - slot
         for j in range(size):
@@ -330,11 +337,10 @@
             rows_ref[j * slots : (j + 1) * slots, :] = patch.astype(BF)
 
     table = jnp.concatenate([table, lane_index.astype(jnp.int32)[None]])
-    width = lifted.shape[1]
     return call_on_blocks(
         body,
         table,
-        [lifted] + mixed + enc_pieces,
+        lifted + mixed + enc_pieces,
         [
             jax.ShapeDtypeStruct((rows, total_rows), F32),
             jax.ShapeDtypeStruct((rows, total_rows), BF),
@@ -587,8 +593,7 @@
 
     if tiled:
         up_t = up_proj.T
-        keys_in, values_in, up_later = lax.optimization_barrier((keys_in, values_in, up_t))
-        lifted_parts = partial_blocks(up_later, enc_pieces)
+        lifted_parts = partial_blocks(up_t, enc_pieces)
         cot_sent = sort_cot(cot_got, patch_total, lane_index)
         cot_mine, cot_other = exchange_pieces(cot_sent)
         cot_packed, table = pack_cot(cot_mine, cot_other, total_rows)
@@ -628,15 +633,9 @@
         queries, *lifted_parts = lax.optimization_barrier((queries, *lifted_parts))
     mixed = attend(queries, keys_in, values_in, member, enc_query.shape[1] // HD)
     if tiled:
-        lifted = scatter_blocks(*lifted_parts).astype(BF)
+        lifted = scatter_blocks(*lifted_parts)
     mixed = jnp.concatenate(gather_mp(mixed), axis=1)
     mixed_pieces = gather_seq(mixed)
-
-    def sum_parts(got):
-        total = got[0].astype(F32)
-        for piece in got[1:]:
-            total = total + piece.astype(F32)
-        return total
 
     rows_of = lambda weight, k: lax.dynamic_slice_in_dim(
         weight, here * slice_width + (lane_index ^ k) * sub, sub, 0
@@ -655,13 +654,13 @@
             lifted, mixed_pieces, enc_pieces, table, lane_index, total_rows, sub
         )
         hidden_pieces = gather_seq(hidden)
-        down_later, _ = lax.optimization_barrier((down_proj, cot_packed))
+        down_later, _ = lax.optimization_barrier((down_proj, mixed[:16]))
         down_t = down_later.T
         forward_blocks = mix_pieces(hidden_pieces, down_t, lane_index)
         forward_got = exchange_mp(forward_blocks)
         down_grad = outer_pieces(cot_all, hidden_pieces, lane_index, scale)
         backward_parts = partial_blocks(down_t, cot_all, lane_index)
-        backward = scatter_blocks(*backward_parts)
+        backward = sum_parts(scatter_blocks(*backward_parts))
         inner = gelu_back(hidden_pre, backward).astype(BF)
         inner_pieces = gather_seq(inner)
         backward_blocks = mix_pieces(inner_pieces, up_t, lane_index)

time: 348 us -> 346 us (level)
  Pallas kernels: 55.1 us -> 45.7 us
  starting transfers between devices: 90.1 us -> 98.9 us
  waiting for transfers between devices: 154 us -> 149 us
  local copies, waits for them, and re-layouts: 26.4 us -> 30.8 us
    pallas_call x2, Pallas kernels: 11.2 us -> 3.86 us  [add_halves(): pl.pallas_call(body, grid=(rows // step,), in_specs=[whole, whole], out_s...]
    ppermute x30, waiting for transfers between devices: 74.5 us -> 68.1 us  [mp_swap(): lax.ppermute(value, 'mp', [(i, i ^ bits) for i in range(lax.axis_size('mp...]
    ppermute x57, starting transfers between devices: 35.8 us -> 41.5 us  [seq_swap(): lax.ppermute(value, 'seq', [(i, i ^ bits) for i in range(lax.axis_size('s...]
    unnamed x141 -> x147, local copies, waits for them, and re-layouts: 18.5 us -> 22.5 us
  transfers between devices with their start and end apart: 87 -> 87, of which waited for: 27 -> 27; matrix products, arithmetic and copies ran while one was open for 8% -> 8% of each run, Pallas kernels for 16% -> 13%
where the time goes in v1:
time: 346 us; the launch traced here: 345 us
  waiting for transfers between devices  149 us (43%)
  starting transfers between devices  98.9 us (29%)
  Pallas kernels  45.7 us (13%)
  local copies, waits for them, and re-layouts  30.8 us (9%)
  matrix products  11.9 us (3%)
  other arithmetic  6.82 us (2%)
    ppermute x57, waiting for transfers between devices, seq_swap(): lax.ppermute(value, 'seq', [(i, i ^ bits) for i in range(lax.axis_size('s...  81 us
    ppermute x30, waiting for transfers between devices, mp_swap(): lax.ppermute(value, 'mp', [(i, i ^ bits) for i in range(lax.axis_size('mp...  68.1 us
    ppermute x30, starting transfers between devices, mp_swap(): lax.ppermute(value, 'mp', [(i, i ^ bits) for i in range(lax.axis_size('mp...  57.4 us
    ppermute x57, starting transfers between devices, seq_swap(): lax.ppermute(value, 'seq', [(i, i ^ bits) for i in range(lax.axis_size('s...  41.5 us
    pallas_call x9, Pallas kernels, call_on_blocks(): pl.pallas_call(body, out_shape=outs, in_specs=[pl.BlockSpec(memory_space=...  23 us
    unnamed x147, local copies, waits for them, and re-layouts  22.5 us
    pallas_call x2, Pallas kernels, mix_pieces(): pl.pallas_call(body, grid_spec=spec, out_shape=[jax.ShapeDtypeStruct((tot...  9.52 us
    pallas_call x2, Pallas kernels, partial_blocks(): pl.pallas_call(body, grid_spec=spec, out_shape=[shape, shape], compiler_p...  9.38 us
  transfers between devices with their start and end apart: 87, of which 27 were waited for; matrix products, arithmetic and copies ran while one was open for 8% of the time, Pallas kernels for 13%

profile of v1, /device:TPU:0, one launch (start us, length us, event | category | flops | bytes accessed | tf_op | source)
XLA Modules:
  0.0 345.4 jit_solution(17318491510671638200)
XLA Ops:
  48.7 4.5 %shard_map.159 = (bf16[4,224,1024]{2,1,0:T(8,128)(2,1)S(1)}, bf16[4,224,1024]{2,1,0:T(8,128)(2,1)}) custom-call(s32[2]{0:T(128)S(1)} %pad_add_fusion.2.place_ref, bf16[1792,512]{1,0:T(8,128)(2,1)S(1)} %bitcast.60, bf16[1792,512]{1,0:T(8,128)(2,1)S(1)} %bitcast.61, bf16[256,512]{1,0:T(8,128)(2,1)S(1)} %constant_dynamic-slice_fusion.11.refs_0_.refs_12_, ...), custom_call_target="tpu_custom_call" | custom-call | flops 1879048192 | bytes 5505024 | tf_op jit(solution)/shard_map/pallas_call | solution.py:175
  55.7 14.2 %collective-permute-done.61.refs_2_ = bf16[1024,128]{1,0:T(8,128)(2,1)S(1)} collective-permute-done((bf16[1024,128]{1,0:T(8,128)(2,1)S(1)}, bf16[1024,128]{1,0:T(8,128)(2,1)S(1)}, u32[]{:S(2)}, u32[]{:S(2)}) %collective-permute-start.61) | collective-permute-done | bytes 262176 | tf_op jit(solution)/shard_map/ppermute | solution.py:57
  71.7 4.8 %shard_map.165 = (bf16[4,224,1024]{2,1,0:T(8,128)(2,1)S(1)}, bf16[4,224,1024]{2,1,0:T(8,128)(2,1)}) custom-call(s32[2]{0:T(128)S(1)} %pad_add_fusion.2.place_ref, bf16[1792,512]{1,0:T(8,128)(2,1)S(1)} %bitcast.63, bf16[1792,512]{1,0:T(8,128)(2,1)S(1)} %bitcast.64, bf16[1024,128]{1,0:T(8,128)(2,1)S(1)} %get-tuple-element.79.refs_0_, ...), custom_call_target="tpu_custom_call" | custom-call | flops 1879048192 | bytes 5505024 | tf_op jit(solution)/shard_map/pallas_call | solution.py:175
  82.4 4.1 %collective-permute-start.18 = (bf16[192,256]{1,0:T(8,128)(2,1)S(1)}, bf16[192,256]{1,0:T(8,128)(2,1)S(1)}, u32[]{:S(2)}, u32[]{:S(2)}) collective-permute-start(bf16[192,256]{1,0:T(8,128)(2,1)S(1)} %copy.38), channel_id=1, source_target_pairs={{0,2},{1,3},{2,0},{3,1},{4,6},{5,7},{6,4},{7,5},{8,10},{9,11},{10,... | collective-permute-start | bytes 294920 | tf_op jit(solution)/shard_map/ppermute | solution.py:57
  87.7 5.6 %collective-permute-start.45 = (bf16[128,512]{1,0:T(8,128)(2,1)S(1)}, bf16[128,512]{1,0:T(8,128)(2,1)S(1)}, u32[]{:S(2)}, u32[]{:S(2)}) collective-permute-start(bf16[128,512]{1,0:T(8,128)(2,1)S(1)} %pad_maximum_fusion.3), channel_id=1, source_target_pairs={{0,2},{1,3},{2,0},{3,1},{4,6},{5,7},{6,4},{7,5},{8,10},{9,11},{10,... | collective-permute-start | bytes 393224 | tf_op jit(solution)/shard_map/ppermute | solution.py:57
  94.9 5.5 %collective-permute-done.17 = bf16[192,256]{1,0:T(8,128)(2,1)S(1)} collective-permute-done((bf16[192,256]{1,0:T(8,128)(2,1)S(1)}, bf16[192,256]{1,0:T(8,128)(2,1)S(1)}, u32[]{:S(2)}, u32[]{:S(2)}) %collective-permute-start.17) | collective-permute-done | bytes 98336 | tf_op jit(solution)/shard_map/ppermute | solution.py:57
  107.8 4.8 %collective-permute-done.21.refs_6_ = bf16[192,1024]{1,0:T(8,128)(2,1)S(1)} collective-permute-done((bf16[192,1024]{1,0:T(8,128)(2,1)S(1)}, bf16[192,1024]{1,0:T(8,128)(2,1)S(1)}, u32[]{:S(2)}, u32[]{:S(2)}) %collective-permute-start.21) | collective-permute-done | bytes 393248 | tf_op jit(solution)/shard_map/ppermute | solution.py:53
  112.6 6.4 %collective-permute-done.23.refs_8_ = bf16[192,1024]{1,0:T(8,128)(2,1)S(1)} collective-permute-done((bf16[192,1024]{1,0:T(8,128)(2,1)S(1)}, bf16[192,1024]{1,0:T(8,128)(2,1)S(1)}, u32[]{:S(2)}, u32[]{:S(2)}) %collective-permute-start.23) | collective-permute-done | bytes 393248 | tf_op jit(solution)/shard_map/ppermute | solution.py:53
  131.0 5.4 %collective-permute-done.14.refs_1_ = bf16[224,1024]{1,0:T(8,128)(2,1)S(1)} collective-permute-done((bf16[224,1024]{1,0:T(8,128)(2,1)S(1)}, bf16[224,1024]{1,0:T(8,128)(2,1)S(1)}, u32[]{:S(2)}, u32[]{:S(2)}) %collective-permute-start.14) | collective-permute-done | bytes 458784 | tf_op jit(solution)/shard_map/ppermute | solution.py:53
  137.9 7.6 %collective-permute-done.15.refs_2_ = bf16[224,1024]{1,0:T(8,128)(2,1)S(1)} collective-permute-done((bf16[224,1024]{1,0:T(8,128)(2,1)S(1)}, bf16[224,1024]{1,0:T(8,128)(2,1)S(1)}, u32[]{:S(2)}, u32[]{:S(2)}) %collective-permute-start.15) | collective-permute-done | bytes 458784 | tf_op jit(solution)/shard_map/ppermute | solution.py:53
  150.0 6.1 %shard_map.161 = (f32[224,1024]{1,0:T(8,128)}, bf16[224,1024]{1,0:T(8,128)(2,1)S(1)}, bf16[1536,128]{1,0:T(8,128)(2,1)S(1)}) custom-call(s32[17]{0:T(128)S(1)} %pad_add_fusion.3.table_ref, f32[224,1024]{1,0:T(8,128)} %copy-done.21, bf16[224,1024]{1,0:T(8,128)(2,1)S(1)} %collective-permute-done.14.refs_1_, ...), custom_call_target="tpu_custom_call" | custom-call | flops 3221225472 | bytes 4521984 | tf_op jit(solution)/shard_map/pallas_call | solution.py:113
  158.9 18.9 %collective-permute-done.50.refs_12_ = bf16[4,128,512]{2,1,0:T(8,128)(2,1)S(1)} collective-permute-done((bf16[4,128,512]{2,1,0:T(8,128)(2,1)S(1)}, bf16[4,128,512]{2,1,0:T(8,128)(2,1)S(1)}, u32[]{:S(2)}, u32[]{:S(2)}) %collective-permute-start.50) | collective-permute-done | bytes 524320 | tf_op jit(solution)/shard_map/ppermute | solution.py:53
  182.1 6.8 %collective-permute-done.65 = bf16[224,1024]{1,0:T(8,128)(2,1)S(1)} collective-permute-done((bf16[224,1024]{1,0:T(8,128)(2,1)S(1)}, bf16[224,1024]{1,0:T(8,128)(2,1)S(1)}, u32[]{:S(2)}, u32[]{:S(2)}) %collective-permute-start.65) | collective-permute-done | bytes 458784 | tf_op jit(solution)/shard_map/ppermute | solution.py:53
  189.4 8.9 %collective-permute-done.64 = bf16[224,1024]{1,0:T(8,128)(2,1)S(1)} collective-permute-done((bf16[224,1024]{1,0:T(8,128)(2,1)S(1)}, bf16[224,1024]{1,0:T(8,128)(2,1)S(1)}, u32[]{:S(2)}, u32[]{:S(2)}) %collective-permute-start.64) | collective-permute-done | bytes 458784 | tf_op jit(solution)/shard_map/ppermute | solution.py:53
  198.3 8.8 %collective-permute-done.30.refs_4_.refs_8_ = bf16[224,1024]{1,0:T(8,128)(2,1)S(1)} collective-permute-done((bf16[224,1024]{1,0:T(8,128)(2,1)S(1)}, bf16[224,1024]{1,0:T(8,128)(2,1)S(1)}, u32[]{:S(2)}, u32[]{:S(2)}) %collective-permute-start.30) | collective-permute-done | bytes 458784 | tf_op jit(solution)/shard_map/ppermute | solution.py:53
  214.8 4.4 %shard_map.162 = (bf16[1024,128]{1,0:T(8,128)(2,1)S(1)}, bf16[1024,128]{1,0:T(8,128)(2,1)S(1)}, bf16[1024,128]{1,0:T(8,128)(2,1)S(1)}, bf16[1024,128]{1,0:T(8,128)(2,1)S(1)}) custom-call(s32[2]{0:T(128)S(1)} %pad_add_fusion.2.place_ref, bf16[1792,512]{1,0:T(8,128)(2,1)S(1)} %bitcast.65, bf16[224,1024]{1,0:T(8,128)(2,1)S(1)} %get-tuple-element.65.refs_0_.refs_4_, ...), custom_call_target="tpu_custom_call" | custom-call | flops 1879048192 | bytes 6553600 | tf_op jit(solution)/shard_map/pallas_call | solution.py:484
  227.5 6.0 %collective-permute-done.70.refs_4_ = bf16[224,1024]{1,0:T(8,128)(2,1)S(1)} collective-permute-done((bf16[224,1024]{1,0:T(8,128)(2,1)S(1)}, bf16[224,1024]{1,0:T(8,128)(2,1)S(1)}, u32[]{:S(2)}, u32[]{:S(2)}) %collective-permute-start.70) | collective-permute-done | bytes 458784 | tf_op jit(solution)/shard_map/ppermute | solution.py:53
  235.0 6.6 %collective-permute-done.35.refs_2_ = bf16[1024,128]{1,0:T(8,128)(2,1)S(1)} collective-permute-done((bf16[1024,128]{1,0:T(8,128)(2,1)S(1)}, bf16[1024,128]{1,0:T(8,128)(2,1)S(1)}, u32[]{:S(2)}, u32[]{:S(2)}) %collective-permute-start.35) | collective-permute-done | bytes 262176 | tf_op jit(solution)/shard_map/ppermute | solution.py:57
  248.6 5.1 %shard_map.167 = (bf16[1024,128]{1,0:T(8,128)(2,1)S(1)}, bf16[1024,128]{1,0:T(8,128)(2,1)}, bf16[1024,128]{1,0:T(8,128)(2,1)S(1)}, bf16[1024,128]{1,0:T(8,128)(2,1)S(1)}) custom-call(s32[2]{0:T(128)S(1)} %pad_add_fusion.2.place_ref, bf16[1792,512]{1,0:T(8,128)(2,1)S(1)} %bitcast.62, bf16[224,1024]{1,0:T(8,128)(2,1)S(1)} %fusion.15.refs_0_, ...), custom_call_target="tpu_custom_call" | custom-call | flops 1879048192 | bytes 6553600 | tf_op jit(solution)/shard_map/pallas_call | solution.py:484
  257.5 4.1 %collective-permute-start.74 = (bf16[1024,128]{1,0:T(8,128)(2,1)}, bf16[1024,128]{1,0:T(8,128)(2,1)S(1)}, u32[]{:S(2)}, u32[]{:S(2)}) collective-permute-start(bf16[1024,128]{1,0:T(8,128)(2,1)} %get-tuple-element.88), channel_id=1, source_target_pairs={{0,1},{1,0},{2,3},{3,2},{4,5},{5,4},{6,7},{7,6},{8,9},{9,8},{10,11... | collective-permute-start | bytes 786440 | tf_op jit(solution)/shard_map/ppermute | solution.py:57
  279.0 13.3 %collective-permute-done.75.refs_2_ = bf16[1024,128]{1,0:T(8,128)(2,1)S(1)} collective-permute-done((bf16[1024,128]{1,0:T(8,128)(2,1)}, bf16[1024,128]{1,0:T(8,128)(2,1)S(1)}, u32[]{:S(2)}, u32[]{:S(2)}) %collective-permute-start.75) | collective-permute-done | bytes 262176 | tf_op jit(solution)/shard_map/ppermute | solution.py:57
  297.5 8.2 %collective-permute-done.55 = bf16[192,512]{1,0:T(8,128)(2,1)S(1)} collective-permute-done((bf16[192,512]{1,0:T(8,128)(2,1)S(1)}, bf16[192,512]{1,0:T(8,128)(2,1)S(1)}, u32[]{:S(2)}, u32[]{:S(2)}) %collective-permute-start.55) | collective-permute-done | bytes 196640 | tf_op jit(solution)/shard_map/ppermute | solution.py:57
  319.0 14.1 %collective-permute-done.84.refs_1_ = bf16[2,192,128]{2,1,0:T(8,128)(2,1)S(1)} collective-permute-done((bf16[2,192,128]{2,1,0:T(8,128)(2,1)S(1)}, bf16[2,192,128]{2,1,0:T(8,128)(2,1)S(1)}, u32[]{:S(2)}, u32[]{:S(2)}) %collective-permute-start.84) | collective-permute-done | bytes 98336 | tf_op jit(solution)/shard_map/ppermute | solution.py:57
  333.7 6.3 %shard_map.171 = bf16[512,1792]{1,0:T(8,128)(2,1)} custom-call(s32[2]{0:T(128)S(1)} %pad_add_fusion.2.place_ref, bf16[1024,128]{1,0:T(8,128)(2,1)S(1)} %copy-done.39, bf16[1024,128]{1,0:T(8,128)(2,1)S(1)} %copy-done.41, bf16[1024,128]{1,0:T(8,128)(2,1)S(1)} %copy-done.43, bf16[1024,128]{1,0:T(8,128)(2,1)S(1)} %copy-done.45, ...), custom_call_target="tpu_custom_call" | custom-call | flops 1879048192 | bytes 6553600 | tf_op jit(solution)/shard_map/pallas_call | solution.py:113
  (357 shorter events, 162.5 us)
Async XLA Ops:
  2.3 41.0 %collective-permute-start.10 = (bf16[256,512]{1,0:T(8,128)(2,1)S(1)}, bf16[256,512]{1,0:T(8,128)(2,1)S(1)}, u32[]{:S(2)}, u32[]{:S(2)}) collective-permute-start(bf16[256,512]{1,0:T(8,128)(2,1)S(1)} %constant_dynamic-slice_fusion.11.refs_0_.refs_12_), channel_id=1, source_target_pairs={{0,1},{1,0},{2,3},{3,2},{4,5},{5,4},{6,7},{7,6},{8,9},{9,8},{10,11... | collective-permute-start | bytes 786440 | tf_op jit(solution)/shard_map/ppermute | solution.py:57
  5.4 40.0 %collective-permute-start.11 = (bf16[256,512]{1,0:T(8,128)(2,1)S(1)}, bf16[256,512]{1,0:T(8,128)(2,1)S(1)}, u32[]{:S(2)}, u32[]{:S(2)}) collective-permute-start(bf16[256,512]{1,0:T(8,128)(2,1)S(1)} %constant_dynamic-slice_fusion.11.refs_0_.refs_12_), channel_id=1, source_target_pairs={{0,2},{1,3},{2,0},{3,1},{4,6},{5,7},{6,4},{7,5},{8,10},{9,11},{10,... | collective-permute-start | bytes 786440 | tf_op jit(solution)/shard_map/ppermute | solution.py:57
  39.6 61.0 %collective-permute-start.46 = (bf16[128,512]{1,0:T(8,128)(2,1)}, bf16[128,512]{1,0:T(8,128)(2,1)}, u32[]{:S(2)}, u32[]{:S(2)}) collective-permute-start(bf16[128,512]{1,0:T(8,128)(2,1)} %pad_maximum_fusion.4), channel_id=1, source_target_pairs={{0,3},{1,2},{2,1},{3,0},{4,7},{5,6},{6,5},{7,4},{8,11},{9,10},{10,... | collective-permute-start | bytes 393224 | tf_op jit(solution)/shard_map/ppermute | solution.py:57
  43.3 26.7 %collective-permute-start.61 = (bf16[1024,128]{1,0:T(8,128)(2,1)S(1)}, bf16[1024,128]{1,0:T(8,128)(2,1)S(1)}, u32[]{:S(2)}, u32[]{:S(2)}) collective-permute-start(bf16[1024,128]{1,0:T(8,128)(2,1)S(1)} %get-tuple-element.79.refs_0_), channel_id=1, source_target_pairs={{0,2},{1,3},{2,0},{3,1},{4,6},{5,7},{6,4},{7,5},{8,10},{9,11},{10,... | collective-permute-start | bytes 786440 | tf_op jit(solution)/shard_map/ppermute | solution.py:57
  54.5 65.0 %collective-permute-start.13 = (bf16[4,224,1024]{2,1,0:T(8,128)(2,1)}, bf16[4,224,1024]{2,1,0:T(8,128)(2,1)}, u32[]{:S(2)}, u32[]{:S(2)}) collective-permute-start(bf16[4,224,1024]{2,1,0:T(8,128)(2,1)} %get-tuple-element.59), channel_id=1, source_target_pairs={{0,4},{4,0},{8,12},{12,8},{16,20},{20,16},{24,28},{28,24},{1,5},{5... | collective-permute-start | bytes 5505032 | tf_op jit(solution)/shard_map/ppermute | solution.py:53
  77.8 49.8 %collective-permute-start.63 = (bf16[4,224,1024]{2,1,0:T(8,128)(2,1)}, bf16[4,224,1024]{2,1,0:T(8,128)(2,1)}, u32[]{:S(2)}, u32[]{:S(2)}) collective-permute-start(bf16[4,224,1024]{2,1,0:T(8,128)(2,1)} %get-tuple-element.81), channel_id=1, source_target_pairs={{0,4},{4,0},{8,12},{12,8},{16,20},{20,16},{24,28},{28,24},{1,5},{5... | collective-permute-start | bytes 5505032 | tf_op jit(solution)/shard_map/ppermute | solution.py:53
  125.3 23.9 %collective-permute-start.16 = (bf16[224,1024]{1,0:T(8,128)(2,1)S(1)}, bf16[224,1024]{1,0:T(8,128)(2,1)S(1)}, u32[]{:S(2)}, u32[]{:S(2)}) collective-permute-start(bf16[224,1024]{1,0:T(8,128)(2,1)S(1)} %get-tuple-element.63), channel_id=1, source_target_pairs={{0,24},{4,28},{8,16},{12,20},{16,8},{20,12},{24,0},{28,4},{1,25},{... | collective-permute-start | bytes 1376264 | tf_op jit(solution)/shard_map/ppermute | solution.py:53
  127.5 28.6 %collective-permute-start.47 = (bf16[4,128,512]{2,1,0:T(8,128)(2,1)S(1)}, bf16[4,128,512]{2,1,0:T(8,128)(2,1)S(1)}, u32[]{:S(2)}, u32[]{:S(2)}) collective-permute-start(bf16[4,128,512]{2,1,0:T(8,128)(2,1)S(1)} %pad_maximum_fusion.refs_8_), channel_id=1, source_target_pairs={{0,4},{4,0},{8,12},{12,8},{16,20},{20,16},{24,28},{28,24},{1,5},{5... | collective-permute-start | bytes 1572872 | tf_op jit(solution)/shard_map/ppermute | solution.py:53
  127.6 29.9 %collective-permute-start.48 = (bf16[4,128,512]{2,1,0:T(8,128)(2,1)S(1)}, bf16[4,128,512]{2,1,0:T(8,128)(2,1)S(1)}, u32[]{:S(2)}, u32[]{:S(2)}) collective-permute-start(bf16[4,128,512]{2,1,0:T(8,128)(2,1)S(1)} %pad_maximum_fusion.refs_8_), channel_id=1, source_target_pairs={{0,8},{4,12},{8,0},{12,4},{16,24},{20,28},{24,16},{28,20},{1,9},{5... | collective-permute-start | bytes 1572872 | tf_op jit(solution)/shard_map/ppermute | solution.py:53
  136.4 41.4 %collective-permute-start.50 = (bf16[4,128,512]{2,1,0:T(8,128)(2,1)S(1)}, bf16[4,128,512]{2,1,0:T(8,128)(2,1)S(1)}, u32[]{:S(2)}, u32[]{:S(2)}) collective-permute-start(bf16[4,128,512]{2,1,0:T(8,128)(2,1)S(1)} %pad_maximum_fusion.refs_8_), channel_id=1, source_target_pairs={{0,16},{4,20},{8,24},{12,28},{16,0},{20,4},{24,8},{28,12},{1,17},{... | collective-permute-start | bytes 1572872 | tf_op jit(solution)/shard_map/ppermute | solution.py:53
  145.5 34.0 %collective-permute-start.52 = (bf16[4,128,512]{2,1,0:T(8,128)(2,1)S(1)}, bf16[4,128,512]{2,1,0:T(8,128)(2,1)S(1)}, u32[]{:S(2)}, u32[]{:S(2)}) collective-permute-start(bf16[4,128,512]{2,1,0:T(8,128)(2,1)S(1)} %pad_maximum_fusion.refs_8_), channel_id=1, source_target_pairs={{0,24},{4,28},{8,16},{12,20},{16,8},{20,12},{24,0},{28,4},{1,25},{... | collective-permute-start | bytes 1572872 | tf_op jit(solution)/shard_map/ppermute | solution.py:53
  149.2 32.9 %collective-permute-start.66 = (bf16[224,1024]{1,0:T(8,128)(2,1)S(1)}, bf16[224,1024]{1,0:T(8,128)(2,1)S(1)}, u32[]{:S(2)}, u32[]{:S(2)}) collective-permute-start(bf16[224,1024]{1,0:T(8,128)(2,1)S(1)} %get-tuple-element.85), channel_id=1, source_target_pairs={{0,24},{4,28},{8,16},{12,20},{16,8},{20,12},{24,0},{28,4},{1,25},{... | collective-permute-start | bytes 1376264 | tf_op jit(solution)/shard_map/ppermute | solution.py:53
  156.1 32.8 %collective-permute-start.65 = (bf16[224,1024]{1,0:T(8,128)(2,1)S(1)}, bf16[224,1024]{1,0:T(8,128)(2,1)S(1)}, u32[]{:S(2)}, u32[]{:S(2)}) collective-permute-start(bf16[224,1024]{1,0:T(8,128)(2,1)S(1)} %get-tuple-element.84), channel_id=1, source_target_pairs={{0,16},{4,20},{8,24},{12,28},{16,0},{20,4},{24,8},{28,12},{1,17},{... | collective-permute-start | bytes 1376264 | tf_op jit(solution)/shard_map/ppermute | solution.py:53
  157.5 31.4 %collective-permute-start.28 = (bf16[224,1024]{1,0:T(8,128)(2,1)S(1)}, bf16[224,1024]{1,0:T(8,128)(2,1)S(1)}, u32[]{:S(2)}, u32[]{:S(2)}) collective-permute-start(bf16[224,1024]{1,0:T(8,128)(2,1)S(1)} %get-tuple-element.65.refs_0_.refs_4_), channel_id=1, source_target_pairs={{0,8},{4,12},{8,0},{12,4},{16,24},{20,28},{24,16},{28,20},{1,9},{5... | collective-permute-start | bytes 1376264 | tf_op jit(solution)/shard_map/ppermute | solution.py:53
  179.6 27.5 %collective-permute-start.30 = (bf16[224,1024]{1,0:T(8,128)(2,1)S(1)}, bf16[224,1024]{1,0:T(8,128)(2,1)S(1)}, u32[]{:S(2)}, u32[]{:S(2)}) collective-permute-start(bf16[224,1024]{1,0:T(8,128)(2,1)S(1)} %get-tuple-element.65.refs_0_.refs_4_), channel_id=1, source_target_pairs={{0,16},{4,20},{8,24},{12,28},{16,0},{20,4},{24,8},{28,12},{1,17},{... | collective-permute-start | bytes 1376264 | tf_op jit(solution)/shard_map/ppermute | solution.py:53
  182.1 26.4 %collective-permute-start.32 = (bf16[224,1024]{1,0:T(8,128)(2,1)S(1)}, bf16[224,1024]{1,0:T(8,128)(2,1)S(1)}, u32[]{:S(2)}, u32[]{:S(2)}) collective-permute-start(bf16[224,1024]{1,0:T(8,128)(2,1)S(1)} %get-tuple-element.65.refs_0_.refs_4_), channel_id=1, source_target_pairs={{0,24},{4,28},{8,16},{12,20},{16,8},{20,12},{24,0},{28,4},{1,25},{... | collective-permute-start | bytes 1376264 | tf_op jit(solution)/shard_map/ppermute | solution.py:53
  262.3 30.0 %collective-permute-start.75 = (bf16[1024,128]{1,0:T(8,128)(2,1)}, bf16[1024,128]{1,0:T(8,128)(2,1)S(1)}, u32[]{:S(2)}, u32[]{:S(2)}) collective-permute-start(bf16[1024,128]{1,0:T(8,128)(2,1)} %copy-done.54), channel_id=1, source_target_pairs={{0,2},{1,3},{2,0},{3,1},{4,6},{5,7},{6,4},{7,5},{8,10},{9,11},{10,... | collective-permute-start | bytes 786440 | tf_op jit(solution)/shard_map/ppermute | solution.py:57
  264.5 27.8 %collective-permute-start.76 = (bf16[1024,128]{1,0:T(8,128)(2,1)}, bf16[1024,128]{1,0:T(8,128)(2,1)S(1)}, u32[]{:S(2)}, u32[]{:S(2)}) collective-permute-start(bf16[1024,128]{1,0:T(8,128)(2,1)} %copy-done.53), channel_id=1, source_target_pairs={{0,3},{1,2},{2,1},{3,0},{4,7},{5,6},{6,5},{7,4},{8,11},{9,10},{10,... | collective-permute-start | bytes 786440 | tf_op jit(solution)/shard_map/ppermute | solution.py:57
  276.4 29.3 %collective-permute-start.55 = (bf16[192,512]{1,0:T(8,128)(2,1)S(1)}, bf16[192,512]{1,0:T(8,128)(2,1)S(1)}, u32[]{:S(2)}, u32[]{:S(2)}) collective-permute-start(bf16[192,512]{1,0:T(8,128)(2,1)S(1)} %get-tuple-element.77), channel_id=1, source_target_pairs={{0,2},{1,3},{2,0},{3,1},{4,6},{5,7},{6,4},{7,5},{8,10},{9,11},{10,... | collective-permute-start | bytes 589832 | tf_op jit(solution)/shard_map/ppermute | solution.py:57
  276.4 29.3 %collective-permute-start.54 = (bf16[192,512]{1,0:T(8,128)(2,1)S(1)}, bf16[192,512]{1,0:T(8,128)(2,1)S(1)}, u32[]{:S(2)}, u32[]{:S(2)}) collective-permute-start(bf16[192,512]{1,0:T(8,128)(2,1)S(1)} %get-tuple-element.76), channel_id=1, source_target_pairs={{0,1},{1,0},{2,3},{3,2},{4,5},{5,4},{6,7},{7,6},{8,9},{9,8},{10,11... | collective-permute-start | bytes 589832 | tf_op jit(solution)/shard_map/ppermute | solution.py:57
  309.6 33.9 %collective-permute-start.59 = (bf16[512,256]{1,0:T(8,128)(2,1)S(1)}, bf16[512,256]{1,0:T(8,128)(2,1)S(1)}, u32[]{:S(2)}, u32[]{:S(2)}) collective-permute-start(bf16[512,256]{1,0:T(8,128)(2,1)S(1)} %get-tuple-element.108), channel_id=1, source_target_pairs={{0,3},{1,2},{2,1},{3,0},{4,7},{5,6},{6,5},{7,4},{8,11},{9,10},{10,... | collective-permute-start | bytes 786440 | tf_op jit(solution)/shard_map/ppermute | solution.py:57
  313.0 30.5 %collective-permute-start.58 = (bf16[512,256]{1,0:T(8,128)(2,1)S(1)}, bf16[512,256]{1,0:T(8,128)(2,1)S(1)}, u32[]{:S(2)}, u32[]{:S(2)}) collective-permute-start(bf16[512,256]{1,0:T(8,128)(2,1)S(1)} %get-tuple-element.109), channel_id=1, source_target_pairs={{0,2},{1,3},{2,0},{3,1},{4,6},{5,7},{6,4},{7,5},{8,10},{9,11},{10,... | collective-permute-start | bytes 786440 | tf_op jit(solution)/shard_map/ppermute | solution.py:57
  313.0 30.5 %collective-permute-start.57 = (bf16[512,256]{1,0:T(8,128)(2,1)S(1)}, bf16[512,256]{1,0:T(8,128)(2,1)S(1)}, u32[]{:S(2)}, u32[]{:S(2)}) collective-permute-start(bf16[512,256]{1,0:T(8,128)(2,1)S(1)} %get-tuple-element.107), channel_id=1, source_target_pairs={{0,1},{1,0},{2,3},{3,2},{4,5},{5,4},{6,7},{7,6},{8,9},{9,8},{10,11... | collective-permute-start | bytes 786440 | tf_op jit(solution)/shard_map/ppermute | solution.py:57
  316.2 25.8 %collective-permute-start.85 = (bf16[2,192,128]{2,1,0:T(8,128)(2,1)S(1)}, bf16[2,192,128]{2,1,0:T(8,128)(2,1)S(1)}, u32[]{:S(2)}, u32[]{:S(2)}) collective-permute-start(bf16[2,192,128]{2,1,0:T(8,128)(2,1)S(1)} %get-tuple-element.97), channel_id=1, source_target_pairs={{0,2},{1,3},{2,0},{3,1},{4,6},{5,7},{6,4},{7,5},{8,10},{9,11},{10,... | collective-permute-start | bytes 294920 | tf_op jit(solution)/shard_map/ppermute | solution.py:57
  (136 other events, 1825.5 us)
